TPU v7x, 32 devices: a whole 2x2x4 slice. The times are simulated.
32 devices in a mesh: ctx: 16 (over z, x, core), tp: 2 (over y).
Axes of the slice: x: 2, y: 2, z: 4, core: 2. Of those that a mesh axis runs over, the one named last changes fastest.
Arguments:
- hidden: bfloat16 [2048, 7168], P('ctx', 'tp'), may hold values from -500 to 500
- embed: bfloat16 [2048, 7168], P('ctx', 'tp'), may hold values from -500 to 500
- gain_hidden: float32 [7168], P('tp'), may hold values from 0.1 to 1.9
- gain_embed: float32 [7168], P('tp'), may hold values from 0.1 to 1.9
- proj_hidden: bfloat16 [7168, 576], P('tp'), may hold values from -0.0625 to 0.0625
- proj_embed: bfloat16 [7168, 576], P('tp'), may hold values from -0.0625 to 0.0625
- gain_latent: float32 [512], replicated, may hold values from 0.1 to 1.9
- key_up: bfloat16 [512, 8192], P(None, 'tp'), may hold values from -0.25 to 0.25
- value_up: bfloat16 [512, 8192], P(None, 'tp'), may hold values from -0.25 to 0.25
- queries: bfloat16 [2048, 12288], P('ctx', 'tp'), may hold values from -60 to 60
- grad_out: bfloat16 [2048, 8192], P('ctx', 'tp'), may hold values from -6 to 6
Outputs:
- attended: bfloat16 [2048, 8192], P('ctx', 'tp')
- grad_queries: bfloat16 [2048, 12288], P('ctx', 'tp')
- grad_hidden: bfloat16 [2048, 7168], P('ctx', 'tp')
- grad_embed: bfloat16 [2048, 7168], P('ctx', 'tp')
All inputs are finite; a program needn't handle non-finite values.
Results may differ from a plain program's by a relative error of at most 0.019.
The roundings to bfloat16 on the way count: a program that leaves them out, or rounds other values in their place, can miss the bound.
Values may be sent and summed in bfloat16 or wider, within the bound.
A program may use at most 192 MiB of HBM per device.

v0:
```python
import jax
import jax.numpy as jnp
from jax import lax
from jax.sharding import PartitionSpec as P

D = 7168
LAT = 512
ROPE = 64
NOPE = 128
VDIM = 128


EPSILON = 1e-06
ROTARY_BASE = 10000.0


def with_halo(x, sides, width):
    for axis, dim in sides:
        size, length = (lax.axis_size(axis), x.shape[dim])
        up = [(i, (i + 1) % size) for i in range(size - 1)]
        down = [(j, i) for i, j in up]
        last = lax.slice_in_dim(x, length - width, length, axis=dim)
        first = lax.slice_in_dim(x, 0, width, axis=dim)
        before = lax.ppermute(last, axis, up)
        after = lax.ppermute(first, axis, down)
        x = jnp.concatenate([before, x, after], axis=dim)
    return x


def rotation(positions):
    pair_count = ROPE // 2
    frequency = ROTARY_BASE ** (-jnp.arange(pair_count, dtype=jnp.float32) / pair_count)
    angles = positions.astype(jnp.float32)[:, None] * frequency[None, :]
    return (jnp.cos(angles), jnp.sin(angles))


def rotate_pairs(values, cos_table, sin_table):
    pair_count = ROPE // 2
    first_half = values[..., :pair_count]
    second_half = values[..., pair_count:]
    return jnp.concatenate(
        [
            first_half * cos_table - second_half * sin_table,
            first_half * sin_table + second_half * cos_table,
        ],
        axis=-1,
    )


def unrotate(values, cos_table, sin_table):
    pair_count = ROPE // 2
    first_half = values[..., :pair_count]
    second_half = values[..., pair_count:]
    return jnp.concatenate(
        [
            first_half * cos_table + second_half * sin_table,
            second_half * cos_table - first_half * sin_table,
        ],
        axis=-1,
    )


def local_positions(tokens, ctx_index, groups):
    half_rows = tokens // 2
    offsets = jnp.arange(tokens, dtype=jnp.int32)
    early_pos = ctx_index * half_rows + offsets
    late_pos = (2 * groups - 1 - ctx_index) * half_rows + offsets - half_rows
    return jnp.where(offsets < half_rows, early_pos, late_pos)


def to_positions(values, groups):
    half_rows = values.shape[0] // (2 * groups)
    trailing = values.shape[1:]
    shaped = values.reshape((groups, 2, half_rows) + trailing)
    early_rows = shaped[:, 0].reshape((groups * half_rows,) + trailing)
    late_rows = shaped[::-1, 1].reshape((groups * half_rows,) + trailing)
    return jnp.concatenate([early_rows, late_rows], axis=0)


def to_rows(values, groups):
    half_rows = values.shape[0] // (2 * groups)
    trailing = values.shape[1:]
    early_rows = values[: groups * half_rows].reshape((groups, half_rows) + trailing)
    late_rows = values[groups * half_rows :].reshape((groups, half_rows) + trailing)[::-1]
    return jnp.stack([early_rows, late_rows], axis=1).reshape((2 * groups * half_rows,) + trailing)


def finish_latent(part_hidden, part_next, squares, gain_latent, positions):
    inverse = lax.rsqrt(squares / D + EPSILON)
    latent = inverse[:, 0:1] * part_hidden + inverse[:, 1:2] * part_next
    leading = latent[:, :LAT]
    inv_latent = lax.rsqrt(jnp.mean(leading * leading, axis=1, keepdims=True) + EPSILON)
    key_latent = (leading * inv_latent * gain_latent).astype(jnp.bfloat16)
    cos_table, sin_table = rotation(positions)
    key_rope = rotate_pairs(latent[:, LAT:], cos_table, sin_table).astype(jnp.bfloat16)
    return (key_latent, key_rope, latent, inverse, inv_latent)


def latent_backward(
    grad_key_latent,
    grad_key_rope,
    latent,
    inverse,
    inv_latent,
    gain_latent,
    positions,
    part_hidden,
    part_next,
):
    cos_table, sin_table = rotation(positions)
    grad_rope = unrotate(grad_key_rope, cos_table, sin_table)
    leading = latent[:, :LAT]
    gained = gain_latent * grad_key_latent
    grad_leading = (
        inv_latent * gained
        - inv_latent**3 * leading * jnp.sum(gained * leading, axis=1, keepdims=True) / LAT
    )
    grad_latent = jnp.concatenate([grad_leading, grad_rope], axis=1)
    part_grad_hidden = (inverse[:, 0:1] * grad_latent).astype(jnp.bfloat16)
    part_grad_next = (inverse[:, 1:2] * grad_latent).astype(jnp.bfloat16)
    inv_sums = jnp.concatenate(
        [
            jnp.sum(grad_latent * part_hidden, axis=1, keepdims=True),
            jnp.sum(grad_latent * part_next, axis=1, keepdims=True),
        ],
        axis=1,
    )
    coefficient = inv_sums * inverse**3 / D
    return (part_grad_hidden, part_grad_next, coefficient)


def attend_half(
    query_rows, grad_rows, query_pos, key_table, block_count, key_block, score_scale, grad_keys
):
    key_total = key_table.shape[0]
    row_total = query_rows.shape[0]
    key_offsets = jnp.arange(key_block, dtype=jnp.int32)

    def score_step(block_index, loop_state):
        buffer, running = loop_state
        first_key = block_index * key_block
        key_slab = lax.dynamic_slice_in_dim(key_table, first_key, key_block, 0)
        scores = (
            jnp.einsum("rc,kc->rk", query_rows, key_slab, preferred_element_type=jnp.float32)
            * score_scale
        )
        allowed = (first_key + key_offsets)[None, :] <= query_pos[:, None]
        scores = jnp.where(allowed, scores, -jnp.inf)
        buffer = lax.dynamic_update_slice_in_dim(buffer, scores, first_key, 1)
        return (buffer, jnp.maximum(running, jnp.max(scores, axis=1)))

    initial = (
        jnp.full((row_total, key_total), -jnp.inf, jnp.float32),
        jnp.full((row_total,), -jnp.inf, jnp.float32),
    )
    buffer, running = lax.fori_loop(0, block_count, score_step, initial)
    weights = jnp.exp(buffer - running[:, None])
    prob_table = (weights / jnp.sum(weights, axis=1, keepdims=True)).astype(jnp.bfloat16)

    def value_step(block_index, running_sum):
        first_key = block_index * key_block
        prob_slab = lax.dynamic_slice_in_dim(prob_table, first_key, key_block, 1)
        value_slab = lax.dynamic_slice_in_dim(key_table, first_key, key_block, 0)[:, :LAT]
        return running_sum + jnp.dot(prob_slab, value_slab, preferred_element_type=jnp.float32)

    out_latent = lax.fori_loop(0, block_count, value_step, jnp.zeros((row_total, LAT), jnp.float32))
    delta_rows = jnp.sum(grad_rows.astype(jnp.float32) * out_latent, axis=1, keepdims=True)

    def grad_step(block_index, loop_state):
        grad_query, grad_keys = loop_state
        first_key = block_index * key_block
        key_slab = lax.dynamic_slice_in_dim(key_table, first_key, key_block, 0)
        prob_slab = lax.dynamic_slice_in_dim(prob_table, first_key, key_block, 1)
        grad_prob = jnp.einsum(
            "rl,kl->rk", grad_rows, key_slab[:, :LAT], preferred_element_type=jnp.float32
        )
        grad_score = (
            prob_slab.astype(jnp.float32) * (grad_prob - delta_rows) * score_scale
        ).astype(jnp.bfloat16)
        grad_query = grad_query + jnp.dot(grad_score, key_slab, preferred_element_type=jnp.float32)
        grad_lead = jnp.einsum(
            "rk,rl->kl", grad_score, query_rows[:, :LAT], preferred_element_type=jnp.float32
        ) + jnp.einsum("rk,rl->kl", prob_slab, grad_rows, preferred_element_type=jnp.float32)
        grad_tail = jnp.einsum(
            "rk,rc->kc", grad_score, query_rows[:, LAT:], preferred_element_type=jnp.float32
        )
        previous = lax.dynamic_slice_in_dim(grad_keys, first_key, key_block, 0)
        update = previous + jnp.concatenate([grad_lead, grad_tail], axis=1)
        return (grad_query, lax.dynamic_update_slice_in_dim(grad_keys, update, first_key, 0))

    grad_query, grad_keys = lax.fori_loop(
        0, block_count, grad_step, (jnp.zeros((row_total, LAT + ROPE), jnp.float32), grad_keys)
    )
    return (out_latent, grad_query, grad_keys)


def on_device(
    hidden,
    embed,
    gain_hidden,
    gain_embed,
    proj_hidden,
    proj_embed,
    gain_latent,
    key_up,
    value_up,
    queries,
    grad_out,
):
    tokens = hidden.shape[0]
    half_rows = tokens // 2
    groups = lax.axis_size("ctx")
    ctx_index = lax.axis_index("ctx")
    head_count = key_up.shape[1] // NOPE
    score_scale = (NOPE + ROPE) ** (-0.5)
    key_total = tokens * groups
    key_block = max(256, key_total // 16)
    edge_rows = jnp.stack([embed[0], embed[half_rows]], axis=0)
    padded = with_halo(edge_rows, (("ctx", 0),), 1)
    after_early = jnp.where(ctx_index == groups - 1, embed[half_rows], padded[3])
    next_embed = jnp.concatenate(
        [embed[1:half_rows], after_early[None], embed[half_rows + 1 :], padded[0][None]], axis=0
    )
    hidden_wide = hidden.astype(jnp.float32)
    next_wide = next_embed.astype(jnp.float32)
    squares = jnp.stack(
        [jnp.sum(hidden_wide * hidden_wide, axis=1), jnp.sum(next_wide * next_wide, axis=1)], axis=1
    )
    scaled_hidden = (hidden_wide * gain_hidden).astype(jnp.bfloat16)
    scaled_next = (next_wide * gain_embed).astype(jnp.bfloat16)
    part_hidden = jnp.dot(scaled_hidden, proj_hidden, preferred_element_type=jnp.float32)
    part_next = jnp.dot(scaled_next, proj_embed, preferred_element_type=jnp.float32)
    positions = local_positions(tokens, ctx_index, groups)
    part_hidden, part_next, squares = lax.psum((part_hidden, part_next, squares), "tp")
    key_latent, key_rope, latent, inverse, inv_latent = finish_latent(
        part_hidden, part_next, squares, gain_latent, positions
    )
    all_latent, all_rope = (
        lax.all_gather(key_latent, "ctx", axis=0, tiled=True),
        lax.all_gather(key_rope, "ctx", axis=0, tiled=True),
    )
    key_table = jnp.concatenate(
        [to_positions(all_latent, groups), to_positions(all_rope, groups)], axis=1
    )
    query_heads = queries.reshape(tokens, head_count, NOPE + ROPE)
    cos_table, sin_table = rotation(positions)
    query_rot = rotate_pairs(
        query_heads[..., NOPE:].astype(jnp.float32), cos_table[:, None], sin_table[:, None]
    ).astype(jnp.bfloat16)
    key_up_heads = key_up.reshape(LAT, head_count, NOPE)
    value_up_heads = value_up.reshape(LAT, head_count, VDIM)
    query_latent = jnp.einsum(
        "shn,lhn->shl", query_heads[..., :NOPE], key_up_heads, preferred_element_type=jnp.float32
    ).astype(jnp.bfloat16)
    query_full = jnp.concatenate([query_latent, query_rot], axis=2)
    grad_latent_rows = jnp.einsum(
        "shv,lhv->shl",
        grad_out.reshape(tokens, head_count, VDIM),
        value_up_heads,
        preferred_element_type=jnp.float32,
    ).astype(jnp.bfloat16)
    grad_keys = jnp.zeros((key_total, LAT + ROPE), jnp.float32)
    attended_parts = []
    grad_query_parts = []
    for segment in range(2):
        if segment == 0:
            first_pos = ctx_index * half_rows
        else:
            first_pos = (2 * groups - 1 - ctx_index) * half_rows
        rows_slice = slice(segment * half_rows, (segment + 1) * half_rows)
        query_rows = query_full[rows_slice].reshape(half_rows * head_count, LAT + ROPE)
        grad_rows = grad_latent_rows[rows_slice].reshape(half_rows * head_count, LAT)
        query_pos = jnp.repeat(first_pos + jnp.arange(half_rows, dtype=jnp.int32), head_count)
        block_count = (first_pos + half_rows + key_block - 1) // key_block
        out_latent, grad_query, grad_keys = attend_half(
            query_rows,
            grad_rows,
            query_pos,
            key_table,
            block_count,
            key_block,
            score_scale,
            grad_keys,
        )
        out_rounded = out_latent.astype(jnp.bfloat16).reshape(half_rows, head_count, LAT)
        attended_parts.append(
            jnp.einsum(
                "shl,lhv->shv", out_rounded, value_up_heads, preferred_element_type=jnp.float32
            ).astype(jnp.bfloat16)
        )
        grad_lead = grad_query[:, :LAT].astype(jnp.bfloat16).reshape(half_rows, head_count, LAT)
        grad_nope = jnp.einsum(
            "shl,lhn->shn", grad_lead, key_up_heads, preferred_element_type=jnp.float32
        )
        grad_rope = unrotate(
            grad_query[:, LAT:].reshape(half_rows, head_count, ROPE),
            cos_table[rows_slice][:, None],
            sin_table[rows_slice][:, None],
        )
        grad_query_parts.append(
            jnp.concatenate([grad_nope, grad_rope], axis=2).astype(jnp.bfloat16)
        )
    attended = jnp.concatenate(attended_parts, axis=0).reshape(tokens, head_count * VDIM)
    grad_queries = jnp.concatenate(grad_query_parts, axis=0).reshape(
        tokens, head_count * (NOPE + ROPE)
    )
    grad_key_rows = to_rows(grad_keys, groups)
    grad_key_latent, grad_key_rope = (
        lax.psum_scatter(grad_key_rows[:, :LAT], "ctx", scatter_dimension=0, tiled=True),
        lax.psum_scatter(grad_key_rows[:, LAT:], "ctx", scatter_dimension=0, tiled=True),
    )
    grad_key_latent, grad_key_rope = lax.psum((grad_key_latent, grad_key_rope), "tp")
    part_grad_hidden, part_grad_next, coefficient = latent_backward(
        grad_key_latent,
        grad_key_rope,
        latent,
        inverse,
        inv_latent,
        gain_latent,
        positions,
        part_hidden,
        part_next,
    )
    grad_hidden = (
        gain_hidden
        * jnp.einsum("rc,dc->rd", part_grad_hidden, proj_hidden, preferred_element_type=jnp.float32)
        - coefficient[:, 0:1] * hidden_wide
    ).astype(jnp.bfloat16)
    grad_next = (
        gain_embed
        * jnp.einsum("rc,dc->rd", part_grad_next, proj_embed, preferred_element_type=jnp.float32)
        - coefficient[:, 1:2] * next_wide
    )
    grad_next_rounded = grad_next.astype(jnp.bfloat16)
    edge_grads = jnp.stack(
        [grad_next_rounded[tokens - 1], grad_next_rounded[half_rows - 1]], axis=0
    )
    returned = with_halo(edge_grads, (("ctx", 0),), 1)
    before_late = jnp.where(ctx_index == groups - 1, grad_next_rounded[half_rows - 1], returned[3])
    grad_embed = jnp.concatenate(
        [
            returned[0][None],
            grad_next_rounded[: half_rows - 1],
            before_late[None],
            grad_next_rounded[half_rows : tokens - 1],
        ],
        axis=0,
    )
    return (attended, grad_queries, grad_hidden, grad_embed)


def solution(mesh):
    placed = (
        P("ctx", "tp"),
        P("ctx", "tp"),
        P("tp"),
        P("tp"),
        P("tp", None),
        P("tp", None),
        P(),
        P(None, "tp"),
        P(None, "tp"),
        P("ctx", "tp"),
        P("ctx", "tp"),
    )
    return jax.shard_map(
        on_device,
        mesh=mesh,
        in_specs=placed,
        out_specs=(P("ctx", "tp"), P("ctx", "tp"), P("ctx", "tp"), P("ctx", "tp")),
        check_vma=False,
    )
```

profile of v0, /device:TPU:0, one launch (start us, length us, event | category | flops | bytes accessed | tf_op | source)
XLA Modules:
  0.0 611.3 jit_solution(14537731783511359108)
XLA Ops:
  24.9 5.9 psum.35
  30.9 29.2 %all-reduce.6.cloned.1.call-done = (f32[128,576]{0,1:T(8,128)}, f32[128,576]{0,1:T(8,128)}) async-done(((f32[128,576]{0,1:T(8,128)}, f32[128,576]{0,1:T(8,128)}), (f32[128,576]{0,1:T(8,128)}, f32[128,576]{0,1:T(8,128)})) %all-reduce.6.cloned.1.call-update) | async-done | bytes 589840 | tf_op jit(solution)/shard_map/psum | solution.py:234
  81.7 5.6 fusion.169
  87.3 6.9 %copy.95 = bf16[64,32,576]{2,1,0:T(8,128)(2,1)} copy(bf16[64,32,576]{0,2,1:T(8,128)(2,1)} %get-tuple-element.453) | data formatting | bytes 4718592 | tf_op jit(solution)/shard_map/slice | solution.py:271
  94.2 22.4 %all_gather.7 = bf16[2048,64]{0,1:T(8,128)(2,1)S(1)} all-gather(bf16[128,64]{0,1:T(8,128)(2,1)S(1)} %pad_maximum_fusion.11), channel_id=1, replica_groups=mesh['ctx'=16,'tp'=2] {'ctx'}, dimensions={0}, use_global_device_ids=true | all-gather | bytes 278528 | tf_op jit(solution)/shard_map/all_gather | solution.py:240
  121.8 6.8 %copy.99 = bf16[64,32,576]{2,1,0:T(8,128)(2,1)} copy(bf16[64,32,576]{0,2,1:T(8,128)(2,1)} %get-tuple-element.454) | data formatting | bytes 4718592 | tf_op jit(solution)/shard_map/slice | solution.py:271
  140.0 7.9 %broadcast.145.clone.1 = f32[2048,2048]{0,1:T(8,128)} broadcast(f32[]{:T(128)} %constant.122.clone.1), dimensions={} | broadcast | bytes 16777220 | tf_op jit(solution)/shard_map/broadcast.18
  152.3 8.1 %fusion.60 = f32[2048]{0:T(1024)S(1)} fusion(f32[2048,2048]{0,1:T(8,128)} %get-tuple-element.246, f32[2048]{0:T(1024)S(1)} %get-tuple-element.247), kind=kLoop, calls=%fused_computation.70 | loop fusion | flops 8386560 | bytes 16793600 | tf_op jit(solution)/shard_map/reduce_sum | solution.py:158
  160.4 9.8 %divide_convert_fusion.1 = bf16[2048,2048]{0,1:T(8,128)(2,1)} fusion(f32[2048,2048]{0,1:T(8,128)} %get-tuple-element.246, f32[2048]{0:T(1024)S(1)} %fusion.60, f32[2048]{0:T(1024)S(1)} %get-tuple-element.247), kind=kLoop, calls=%fused_computation.68 | loop fusion | flops 12582912 | bytes 25182208 | tf_op jit(solution)/shard_map/convert_element_type | solution.py:158
  178.1 6.1 multiply_reduce_fusion.1
  189.6 14.0 %while.72 = (s32[]{:T(128)}, f32[2048,576]{0,1:T(8,128)}, f32[2048,576]{1,0:T(8,128)}, s32[]{:T(128)}, bf16[2048,2048]{0,1:T(8,128)(2,1)}, /*index=5*/bf16[2048,...) while((s32[]{:T(128)}, f32[2048,576]{0,1:T(8,128)}, ...), condition=%wide.region_20.21_spmd, body=%wide.region_19.20_spmd.sunk | while | flops 2285928448 | bytes 44508400 | solution.py:191
  203.6 7.9 %broadcast.145.clone = f32[2048,2048]{0,1:T(8,128)} broadcast(f32[]{:T(128)} %constant.122.clone.1), dimensions={} | broadcast | bytes 16777220 | tf_op jit(solution)/shard_map/broadcast.18
  211.5 35.3 %while.75 = (s32[]{:T(128)}, f32[2048,2048]{0,1:T(8,128)}, f32[2048]{0:T(1024)S(1)}, s32[]{:T(128)}, bf16[2048,576]{1,0:T(8,128)(2,1)}, /*index=5*/bf16[2048,576...) while((s32[]{:T(128)}, f32[2048,2048]{0,1:T(8,128)}, ...), condition=%wide.region_14.15_spmd.clone, body=%wide.region_12.14_spmd.clone.sunk | while | flops 606077184 | bytes 5115295 | solution.py:156
  246.8 8.1 %fusion.61 = f32[2048]{0:T(1024)S(1)} fusion(f32[2048,2048]{0,1:T(8,128)} %get-tuple-element.249, f32[2048]{0:T(1024)S(1)} %get-tuple-element.250), kind=kLoop, calls=%fused_computation.71 | loop fusion | flops 8386560 | bytes 16793600 | tf_op jit(solution)/shard_map/reduce_sum | solution.py:158
  254.8 9.8 %divide_convert_fusion = bf16[2048,2048]{0,1:T(8,128)(2,1)} fusion(f32[2048,2048]{0,1:T(8,128)} %get-tuple-element.249, f32[2048]{0:T(1024)S(1)} %fusion.61, f32[2048]{0:T(1024)S(1)} %get-tuple-element.250), kind=kLoop, calls=%fused_computation.66 | loop fusion | flops 12582912 | bytes 25182208 | tf_op jit(solution)/shard_map/convert_element_type | solution.py:158
  267.2 42.7 %while.71 = (s32[]{:T(128)}, f32[2048,512]{1,0:T(8,128)}, s32[]{:T(128)}, bf16[2048,2048]{0,1:T(8,128)(2,1)}, bf16[2048,576]{1,0:T(8,128)(2,1)}, /*index=5*/s32[]{:T(128)}, s32[]{:T(128)}, s32[]{:T(128)}, s32[]{:T(128)}) while((s32[]{:T(128)}, f32[2048,512]{1,0:T(8,128)}, s32[]{:T(128)}, bf16[2048,2048]{0,1:T(8,128)(2,1)}, ...), condition=%wide.region_17.18_spmd, body=%wide.region_16.17_spmd.sunk | while | flops 537919488 | bytes 9700491 | solution.py:166
  309.9 5.5 multiply_reduce_fusion
  318.1 103.3 %while.73 = (s32[]{:T(128)}, f32[2048,576]{0,1:T(8,128)}, f32[2048,576]{1,0:T(8,128)}, s32[]{:T(128)}, bf16[2048,2048]{0,1:T(8,128)(2,1)}, /*index=5*/bf16[2048,...) while((s32[]{:T(128)}, f32[2048,576]{0,1:T(8,128)}, ...), condition=%wide.region_23.24_spmd, body=%wide.region_22.23_spmd.sunk | while | flops 2285928448 | bytes 36119764 | solution.py:191
  437.9 5.9 copy.111
  448.0 6.0 copy.121
  494.3 11.3 %reduce-scatter.3.cloned.1.call-done = f32[128,512]{0,1:T(8,128)} async-done(((f32[2048,512]{0,1:T(8,128)}), f32[128,512]{0,1:T(8,128)}) %reduce-scatter.3.cloned.1.call-update) | async-done | bytes 262160 | tf_op jit(solution)/shard_map/reduce_scatter | solution.py:309
  507.9 56.4 %reduce-scatter.5.cloned.1.call-done = f32[128,64]{0,1:T(8,128)} async-done(((f32[2048,64]{0,1:T(8,128)}), f32[128,64]{0,1:T(8,128)}) %reduce-scatter.5.cloned.1.call-update) | async-done | bytes 32784 | tf_op jit(solution)/shard_map/reduce_scatter | solution.py:310
  564.3 9.1 %psum.39 = f32[128,64]{0,1:T(8,128)S(1)} all-reduce(f32[128,64]{0,1:T(8,128)} %reduce-scatter.5.cloned.1.call-done), channel_id=1, replica_groups=mesh['ctx'=16,'tp'=2] {'tp'}, use_global_device_ids=true, to_apply=%region_28.29 | all-reduce | flops 8192 | bytes 65536 | tf_op jit(solution)/shard_map/psum | solution.py:312
  573.6 15.2 %all-reduce.4.cloned.1.call-done = f32[128,512]{0,1:T(8,128)} async-done(((f32[128,512]{0,1:T(8,128)}), f32[128,512]{0,1:T(8,128)}) %all-reduce.4.cloned.1.call-update) | async-done | bytes 262160 | tf_op jit(solution)/shard_map/psum | solution.py:312
  (342 shorter events, 361.0 us)
Async XLA Ops:
  7.2 52.9 %all-reduce.6.cloned.1.call-start = ((), (), s32[]{:S(2)}) async-start(), calls=%async_computation.6 | async-start | bytes 1179648 | tf_op jit(solution)/shard_map/psum | solution.py:234
  8.1 7.5 %collective-permute-start = (bf16[1,3584]{1,0:T(2,128)(2,1)S(1)}, bf16[1,3584]{1,0:T(2,128)(2,1)S(1)}, u32[]{:S(2)}, u32[]{:S(2)}) collective-permute-start(bf16[1,3584]{1,0:T(2,128)(2,1)S(1)} %slice.171), channel_id=1, source_target_pairs={{2,0},{4,2},{6,4},{8,6},{10,8},{12,10},{14,12},{16,14},{18,16},{20... | collective-permute-start | bytes 21512 | tf_op jit(solution)/shard_map/ppermute | solution.py:25
  16.5 3.9 collective-permute-start.1
  24.5 104.1 %all-gather.2.cloned.1.call-start = ((), (), s32[]{:S(2)}) async-start(), calls=%async_computation.2 | async-start | bytes 2228224 | tf_op jit(solution)/shard_map/all_gather | solution.py:239
  62.7 443.0 %reduce-scatter.3.cloned.1.call-start = ((), (), s32[]{:S(2)}) async-start(), calls=%async_computation.3 | async-start | bytes 4456448 | tf_op jit(solution)/shard_map/reduce_scatter | solution.py:309
  435.5 128.8 %reduce-scatter.5.cloned.1.call-start = ((), (), s32[]{:S(2)}) async-start(), calls=%async_computation.5 | async-start | bytes 557056 | tf_op jit(solution)/shard_map/reduce_scatter | solution.py:310
  488.4 100.4 %all-reduce.4.cloned.1.call-start = ((), (), s32[]{:S(2)}) async-start(), calls=%async_computation.4 | async-start | bytes 524288 | tf_op jit(solution)/shard_map/psum | solution.py:312
  505.8 67.7 %copy-start.44 = (f32[128]{0:T(128)S(1)}, f32[128]{0:T(128)}, u32[]{:S(2)}) copy-start(f32[128]{0:T(128)} %copy-done.43) | copy-start | bytes 1540
  505.8 67.7 %copy-start.46 = (f32[32]{0:T(128)S(1)}, f32[32]{0:T(128)}, u32[]{:S(2)}) copy-start(f32[32]{0:T(128)} %copy-done.45) | copy-start | bytes 388
  505.8 83.0 %copy-start.8 = (f32[128,576]{0,1:T(8,128)S(1)}, f32[128,576]{0,1:T(8,128)}, u32[]{:S(2)}) copy-start(f32[128,576]{0,1:T(8,128)} %copy-done.7) | copy-start | bytes 884740
  505.8 83.0 %copy-start.34 = (f32[512]{0:T(512)S(1)}, f32[512]{0:T(512)}, u32[]{:S(2)}) copy-start(f32[512]{0:T(512)} %param.29) | copy-start | bytes 6148
  505.8 84.1 %copy-start.48 = (f32[128]{0:T(128)S(1)}, f32[128]{0:T(128)}, u32[]{:S(2)}) copy-start(f32[128]{0:T(128)} %copy-done.47) | copy-start | bytes 1540
  505.8 84.1 %copy-start.49 = (f32[128]{0:T(128)S(1)}, f32[128]{0:T(128)}, u32[]{:S(2)}) copy-start(f32[128]{0:T(128)} %get-tuple-element.499) | copy-start | bytes 1540
  505.8 85.2 %copy-start.22 = (f32[128,576]{0,1:T(8,128)S(1)}, f32[128,576]{0,1:T(8,128)}, u32[]{:S(2)}) copy-start(f32[128,576]{0,1:T(8,128)} %get-tuple-element.445) | copy-start | bytes 884740
  505.8 85.2 %copy-start.23 = (f32[128,576]{0,1:T(8,128)S(1)}, f32[128,576]{0,1:T(8,128)}, u32[]{:S(2)}) copy-start(f32[128,576]{0,1:T(8,128)} %get-tuple-element.446) | copy-start | bytes 884740
  506.5 84.6 %copy-start.38 = (f32[128,2]{0,1:T(2,128)S(1)}, f32[128,2]{0,1:T(2,128)}, u32[]{:S(2)}) copy-start(f32[128,2]{0,1:T(2,128)} %copy-done.37) | copy-start | bytes 3076
  506.5 84.6 %copy-start.19 = (bf16[63,3584]{1,0:T(8,128)(2,1)S(1)}, bf16[63,3584]{1,0:T(8,128)(2,1)}, u32[]{:S(2)}) copy-start(bf16[63,3584]{1,0:T(8,128)(2,1)} %copy-done.18) | copy-start | bytes 1354756
  506.5 84.6 %copy-start.21 = (bf16[63,3584]{1,0:T(8,128)(2,1)S(1)}, bf16[63,3584]{1,0:T(8,128)(2,1)}, u32[]{:S(2)}) copy-start(bf16[63,3584]{1,0:T(8,128)(2,1)} %copy-done.20) | copy-start | bytes 1354756
  506.5 84.6 %copy-start.32 = (bf16[1,3584]{1,0:T(2,128)(2,1)S(1)}, bf16[1,3584]{1,0:T(2,128)(2,1)}, u32[]{:S(2)}) copy-start(bf16[1,3584]{1,0:T(2,128)(2,1)} %copy-done.31) | copy-start | bytes 21508
  506.5 84.6 %copy-start.36 = (bf16[1,3584]{1,0:T(2,128)(2,1)S(1)}, bf16[1,3584]{1,0:T(2,128)(2,1)}, u32[]{:S(2)}) copy-start(bf16[1,3584]{1,0:T(2,128)(2,1)} %copy-done.35) | copy-start | bytes 21508
  506.6 84.6 %copy-start.42 = (f32[128]{0:T(128)S(1)}, f32[128]{0:T(128)}, u32[]{:S(2)}) copy-start(f32[128]{0:T(128)} %copy-done.41) | copy-start | bytes 1540
  506.6 84.6 %copy-start.51 = (f32[3584]{0:T(1024)S(1)}, f32[3584]{0:T(1024)}, u32[]{:S(2)}) copy-start(f32[3584]{0:T(1024)} %param.26) | copy-start | bytes 43012
  594.6 3.1 collective-permute-start.3
  597.7 5.6 collective-permute-start.2
  (46 other events, 432.4 us)
Sparse Core Ops, SparseCore 0:
  24.6 35.3 all-reduce.5
  62.8 41.3 all-gather.1
  435.6 69.9 reduce-scatter.2
  509.0 55.2 reduce-scatter.4
  566.4 22.3 all-reduce.3
where the time goes:
time: 617 us; the launch traced here: 611 us
  matrix products  221 us (36%)
  local copies, waits for them, and re-layouts  128 us (21%)
  waiting for transfers between devices  114 us (18%)
  other arithmetic  84.5 us (14%)
  blocking collectives  37.4 us (6%)
  between operations  15 us (2%)
  starting transfers between devices  9.95 us (2%)
    reduce_scatter x1, waiting for transfers between devices, on_device(): lax.psum_scatter(grad_key_rows[:, LAT:], 'ctx', scatter_dimension=0, tile...  56.4 us
    dot_general x9, matrix products, grad_step(): jnp.dot(grad_score, key_slab, preferred_element_type=jnp.float32)  49.1 us
    dot_general x9, matrix products, value_step(): jnp.dot(prob_slab, value_slab, preferred_element_type=jnp.float32)  48 us
    dot_general x9, matrix products, score_step(): jnp.einsum('rc,kc->rk', query_rows, key_slab, preferred_element_type=jnp....  38.3 us
    psum x1, waiting for transfers between devices, on_device(): lax.psum((part_hidden, part_next, squares), 'tp')  29.2 us
    another operation x9, local copies, waits for them, and re-layouts  29.1 us
    all_gather x1, blocking collectives, on_device(): lax.all_gather(key_rope, 'ctx', axis=0, tiled=True)  22.4 us
    convert_element_type x2, other arithmetic, attend_half(): (weights / jnp.sum(weights, axis=1, keepdims=True)).astype(jnp.bfloat16)  19.7 us
  transfers between devices with their start and end apart: 9, of which 6 were waited for; matrix products, arithmetic and copies ran while one was open for 18% of the time, Pallas kernels for 0%

commit v1 on v0

v1 whole, which is shorter than its diff:
```python
import functools

import jax
import jax.numpy as jnp
from jax import lax
from jax.experimental import pallas as pl
from jax.experimental.pallas import tpu as pltpu
from jax.sharding import PartitionSpec as P

D = 7168
LAT = 512
ROPE = 64
NOPE = 128
VDIM = 128


EPSILON = 1e-06
ROTARY_BASE = 10000.0


def with_halo(x, sides, width):
    for axis, dim in sides:
        size, length = (lax.axis_size(axis), x.shape[dim])
        up = [(i, (i + 1) % size) for i in range(size - 1)]
        down = [(j, i) for i, j in up]
        last = lax.slice_in_dim(x, length - width, length, axis=dim)
        first = lax.slice_in_dim(x, 0, width, axis=dim)
        before = lax.ppermute(last, axis, up)
        after = lax.ppermute(first, axis, down)
        x = jnp.concatenate([before, x, after], axis=dim)
    return x


def rotation(positions):
    pair_count = ROPE // 2
    frequency = ROTARY_BASE ** (-jnp.arange(pair_count, dtype=jnp.float32) / pair_count)
    angles = positions.astype(jnp.float32)[:, None] * frequency[None, :]
    return (jnp.cos(angles), jnp.sin(angles))


def rotate_pairs(values, cos_table, sin_table):
    pair_count = ROPE // 2
    first_half = values[..., :pair_count]
    second_half = values[..., pair_count:]
    return jnp.concatenate(
        [
            first_half * cos_table - second_half * sin_table,
            first_half * sin_table + second_half * cos_table,
        ],
        axis=-1,
    )


def unrotate(values, cos_table, sin_table):
    pair_count = ROPE // 2
    first_half = values[..., :pair_count]
    second_half = values[..., pair_count:]
    return jnp.concatenate(
        [
            first_half * cos_table + second_half * sin_table,
            second_half * cos_table - first_half * sin_table,
        ],
        axis=-1,
    )


def local_positions(tokens, ctx_index, groups):
    half_rows = tokens // 2
    offsets = jnp.arange(tokens, dtype=jnp.int32)
    early_pos = ctx_index * half_rows + offsets
    late_pos = (2 * groups - 1 - ctx_index) * half_rows + offsets - half_rows
    return jnp.where(offsets < half_rows, early_pos, late_pos)


def finish_latent(part_hidden, part_next, squares, gain_latent, positions):
    inverse = lax.rsqrt(squares / D + EPSILON)
    latent = inverse[:, 0:1] * part_hidden + inverse[:, 1:2] * part_next
    leading = latent[:, :LAT]
    inv_latent = lax.rsqrt(jnp.mean(leading * leading, axis=1, keepdims=True) + EPSILON)
    key_latent = (leading * inv_latent * gain_latent).astype(jnp.bfloat16)
    cos_table, sin_table = rotation(positions)
    key_rope = rotate_pairs(latent[:, LAT:], cos_table, sin_table).astype(jnp.bfloat16)
    return (key_latent, key_rope, latent, inverse, inv_latent)


def latent_backward(
    grad_key_latent,
    grad_key_rope,
    latent,
    inverse,
    inv_latent,
    gain_latent,
    positions,
    part_hidden,
    part_next,
):
    cos_table, sin_table = rotation(positions)
    grad_rope = unrotate(grad_key_rope, cos_table, sin_table)
    leading = latent[:, :LAT]
    gained = gain_latent * grad_key_latent
    grad_leading = (
        inv_latent * gained
        - inv_latent**3 * leading * jnp.sum(gained * leading, axis=1, keepdims=True) / LAT
    )
    grad_latent = jnp.concatenate([grad_leading, grad_rope], axis=1)
    part_grad_hidden = (inverse[:, 0:1] * grad_latent).astype(jnp.bfloat16)
    part_grad_next = (inverse[:, 1:2] * grad_latent).astype(jnp.bfloat16)
    inv_sums = jnp.concatenate(
        [
            jnp.sum(grad_latent * part_hidden, axis=1, keepdims=True),
            jnp.sum(grad_latent * part_next, axis=1, keepdims=True),
        ],
        axis=1,
    )
    coefficient = inv_sums * inverse**3 / D
    return (part_grad_hidden, part_grad_next, coefficient)


def group_size(head_count):
    for size in (4, 2, 1):
        if head_count % size == 0:
            return size


def attention_kernel(
    groups,
    group,
    key_block,
    score_scale,
    keys_ref,
    queries_ref,
    grad_out_ref,
    key_up_ref,
    value_up_ref,
    cos_ref,
    sin_ref,
    attended_ref,
    grad_queries_ref,
    grad_keys_ref,
    table,
    table_t,
    query_rows,
    grad_rows,
    score_buf,
    dprob_buf,
    out_acc,
    dquery_acc,
    dkey_acc,
):
    step = pl.program_id(0)
    ctx_index = lax.axis_index("ctx")
    tokens = queries_ref.shape[0]
    half_rows = tokens // 2
    rows = group * half_rows
    key_total = keys_ref.shape[0]
    width = LAT + ROPE
    padded = table.shape[1]
    blocks = key_total // key_block
    chunk_rows = [
        (2 * c if c < groups else 2 * (2 * groups - 1 - c) + 1) * half_rows
        for c in range(2 * groups)
    ]

    @pl.when(step == 0)
    def _():
        dkey_acc[...] = jnp.zeros_like(dkey_acc)
        query_rows[...] = jnp.zeros_like(query_rows)
        for c, row in enumerate(chunk_rows):
            chunk = keys_ref[row : row + half_rows, :]
            pad = jnp.zeros((half_rows, padded - width), chunk.dtype)
            table[c * half_rows : (c + 1) * half_rows, :] = jnp.concatenate([chunk, pad], axis=1)

        @pl.loop(0, blocks)
        def _(j):
            first = pl.multiple_of(j * key_block, key_block)
            table_t[j] = table[pl.ds(first, key_block), :].T

    cos2 = cos_ref[...]
    sin2 = sin_ref[...]
    half = ROPE // 2
    nt = (((1,), (1,)), ((), ()))
    tn = (((0,), (0,)), ((), ()))
    all_queries = queries_ref[...]
    for g in range(group):
        first = g * (NOPE + ROPE)
        nope = all_queries[:, first : first + NOPE]
        rope = all_queries[:, first + NOPE : first + NOPE + ROPE].astype(jnp.float32)
        swapped = jnp.concatenate([-rope[:, half:], rope[:, :half]], axis=1)
        rotated = (rope * cos2 + swapped * sin2).astype(jnp.bfloat16)
        lead = lax.dot_general(
            nope, key_up_ref[:, g * NOPE : (g + 1) * NOPE], nt, preferred_element_type=jnp.float32
        ).astype(jnp.bfloat16)
        grads = lax.dot_general(
            grad_out_ref[:, g * VDIM : (g + 1) * VDIM],
            value_up_ref[:, g * VDIM : (g + 1) * VDIM],
            nt,
            preferred_element_type=jnp.float32,
        ).astype(jnp.bfloat16)
        for h in range(2):
            source = slice(h * half_rows, (h + 1) * half_rows)
            target = slice(g * half_rows, (g + 1) * half_rows)
            query_rows[h, target, :LAT] = lead[source]
            query_rows[h, target, LAT : LAT + ROPE] = rotated[source]
            grad_rows[h, target, :] = grads[source]

    for h in range(2):
        first_pos = (ctx_index if h == 0 else 2 * groups - 1 - ctx_index) * half_rows
        block_count = (first_pos + half_rows + key_block - 1) // key_block
        row_pos = first_pos + lax.broadcasted_iota(jnp.int32, (rows, key_block), 0) % half_rows
        key_off = lax.broadcasted_iota(jnp.int32, (rows, key_block), 1)
        gap = row_pos - key_off
        lanes = 128

        def fold(values, op):
            total = values[:, :lanes]
            for k in range(1, key_block // lanes):
                total = op(total, values[:, k * lanes : (k + 1) * lanes])
            return total

        def score_step(j, running):
            scores = jnp.dot(query_rows[h], table_t[j], preferred_element_type=jnp.float32)
            scores = jnp.where(gap >= j * key_block, scores, -1e30)
            score_buf[j] = scores
            dprob_buf[j] = jnp.dot(
                grad_rows[h], table_t[j, :LAT, :], preferred_element_type=jnp.float32
            )
            return jnp.maximum(running, fold(scores, jnp.maximum))

        running = lax.fori_loop(
            0, block_count, score_step, jnp.full((rows, lanes), -1e30, jnp.float32)
        )
        row_max = jnp.max(running, axis=1, keepdims=True)

        def weight_step(j, sums):
            weights = jnp.exp((score_buf[j] - row_max) * score_scale)
            score_buf[j] = weights
            return (
                sums[0] + fold(weights, jnp.add),
                sums[1] + fold(weights * dprob_buf[j], jnp.add),
            )

        zeros = jnp.zeros((rows, lanes), jnp.float32)
        weight_sum, delta_sum = lax.fori_loop(0, block_count, weight_step, (zeros, zeros))
        inv_sum = 1.0 / jnp.sum(weight_sum, axis=1, keepdims=True)
        delta = jnp.sum(delta_sum, axis=1, keepdims=True) * inv_sum
        out_acc[...] = jnp.zeros_like(out_acc)
        dquery_acc[...] = jnp.zeros_like(dquery_acc)

        def grad_step(j, carry):
            first = pl.multiple_of(j * key_block, key_block)
            prob = (score_buf[j] * inv_sum).astype(jnp.bfloat16)
            dscore = (
                prob.astype(jnp.float32) * (dprob_buf[j] - delta) * score_scale
            ).astype(jnp.bfloat16)
            keys = table[pl.ds(first, key_block), :]
            out_acc[...] += jnp.dot(prob, keys[:, :LAT], preferred_element_type=jnp.float32)
            dquery_acc[...] += jnp.dot(dscore, keys, preferred_element_type=jnp.float32)
            dkey_acc[pl.ds(first, key_block), :] += lax.dot_general(
                dscore, query_rows[h], tn, preferred_element_type=jnp.float32
            )
            dkey_acc[pl.ds(first, key_block), :LAT] += lax.dot_general(
                prob, grad_rows[h], tn, preferred_element_type=jnp.float32
            )
            return carry

        lax.fori_loop(0, block_count, grad_step, 0)
        token = slice(h * half_rows, (h + 1) * half_rows)
        pieces = []
        for g in range(group):
            part = slice(g * half_rows, (g + 1) * half_rows)
            attended_ref[token, g * VDIM : (g + 1) * VDIM] = jnp.dot(
                out_acc[part, :].astype(jnp.bfloat16),
                value_up_ref[:, g * VDIM : (g + 1) * VDIM],
                preferred_element_type=jnp.float32,
            ).astype(jnp.bfloat16)
            pieces.append(
                jnp.dot(
                    dquery_acc[part, :LAT].astype(jnp.bfloat16),
                    key_up_ref[:, g * NOPE : (g + 1) * NOPE],
                    preferred_element_type=jnp.float32,
                )
            )
            tail = dquery_acc[part, LAT : LAT + ROPE]
            swapped = jnp.concatenate([tail[:, half:], -tail[:, :half]], axis=1)
            pieces.append(tail * cos2[token] + swapped * sin2[token])
        grad_queries_ref[token, :] = jnp.concatenate(pieces, axis=1).astype(jnp.bfloat16)

    @pl.when(step == pl.num_programs(0) - 1)
    def _():
        for c, row in enumerate(chunk_rows):
            grad_keys_ref[row : row + half_rows, :] = dkey_acc[
                c * half_rows : (c + 1) * half_rows, :width
            ].astype(grad_keys_ref.dtype)


def attention(keys, queries, grad_out, key_up, value_up, cos2, sin2, groups):
    tokens = queries.shape[0]
    half_rows = tokens // 2
    head_count = key_up.shape[1] // NOPE
    group = group_size(head_count)
    key_total = keys.shape[0]
    key_block = 256
    blocks = key_total // key_block
    padded = LAT + 2 * ROPE
    rows = group * half_rows
    body = functools.partial(
        attention_kernel, groups, group, key_block, (NOPE + ROPE) ** (-0.5)
    )
    whole = lambda shape: pl.BlockSpec(shape, lambda i: (0, 0), pipeline_mode=pl.Buffered(1))
    column = lambda height, width: pl.BlockSpec((height, group * width), lambda i: (0, i))
    return pl.pallas_call(
        body,
        grid=(head_count // group,),
        in_specs=[
            whole(keys.shape),
            column(tokens, NOPE + ROPE),
            column(tokens, VDIM),
            column(LAT, NOPE),
            column(LAT, VDIM),
            whole(cos2.shape),
            whole(sin2.shape),
        ],
        out_specs=[
            column(tokens, VDIM),
            column(tokens, NOPE + ROPE),
            whole(keys.shape),
        ],
        out_shape=[
            jax.ShapeDtypeStruct((tokens, head_count * VDIM), jnp.bfloat16),
            jax.ShapeDtypeStruct((tokens, head_count * (NOPE + ROPE)), jnp.bfloat16),
            jax.ShapeDtypeStruct(keys.shape, jnp.bfloat16),
        ],
        scratch_shapes=[
            pltpu.VMEM((key_total, padded), jnp.bfloat16),
            pltpu.VMEM((blocks, padded, key_block), jnp.bfloat16),
            pltpu.VMEM((2, rows, padded), jnp.bfloat16),
            pltpu.VMEM((2, rows, LAT), jnp.bfloat16),
            pltpu.VMEM((blocks, rows, key_block), jnp.float32),
            pltpu.VMEM((blocks, rows, key_block), jnp.float32),
            pltpu.VMEM((rows, LAT), jnp.float32),
            pltpu.VMEM((rows, padded), jnp.float32),
            pltpu.VMEM((key_total, padded), jnp.float32),
        ],
        compiler_params=pltpu.CompilerParams(
            dimension_semantics=("arbitrary",), vmem_limit_bytes=60 * 1024 * 1024
        ),
        name="attention",
    )(keys, queries, grad_out, key_up, value_up, cos2, sin2)


def pair_sum(values):
    if lax.axis_size("tp") != 2:
        return lax.psum(values, "tp")
    return tuple(v + lax.ppermute(v, "tp", [(0, 1), (1, 0)]) for v in values)


def on_device(
    hidden,
    embed,
    gain_hidden,
    gain_embed,
    proj_hidden,
    proj_embed,
    gain_latent,
    key_up,
    value_up,
    queries,
    grad_out,
):
    tokens = hidden.shape[0]
    half_rows = tokens // 2
    groups = lax.axis_size("ctx")
    ctx_index = lax.axis_index("ctx")
    edge_rows = jnp.stack([embed[0], embed[half_rows]], axis=0)
    padded = with_halo(edge_rows, (("ctx", 0),), 1)
    after_early = jnp.where(ctx_index == groups - 1, embed[half_rows], padded[3])
    next_embed = jnp.concatenate(
        [embed[1:half_rows], after_early[None], embed[half_rows + 1 :], padded[0][None]], axis=0
    )
    hidden_wide = hidden.astype(jnp.float32)
    next_wide = next_embed.astype(jnp.float32)
    squares = jnp.stack(
        [jnp.sum(hidden_wide * hidden_wide, axis=1), jnp.sum(next_wide * next_wide, axis=1)], axis=1
    )
    scaled_hidden = (hidden_wide * gain_hidden).astype(jnp.bfloat16)
    scaled_next = (next_wide * gain_embed).astype(jnp.bfloat16)
    part_hidden = jnp.dot(scaled_hidden, proj_hidden, preferred_element_type=jnp.float32)
    part_next = jnp.dot(scaled_next, proj_embed, preferred_element_type=jnp.float32)
    positions = local_positions(tokens, ctx_index, groups)
    part_hidden, part_next, squares = pair_sum((part_hidden, part_next, squares))
    key_latent, key_rope, latent, inverse, inv_latent = finish_latent(
        part_hidden, part_next, squares, gain_latent, positions
    )
    keys = lax.all_gather(
        jnp.concatenate([key_latent, key_rope], axis=1), "ctx", axis=0, tiled=True
    )
    cos_table, sin_table = rotation(positions)
    attended, grad_queries, grad_keys = attention(
        keys,
        queries,
        grad_out,
        key_up,
        value_up,
        jnp.concatenate([cos_table, cos_table], axis=1),
        jnp.concatenate([sin_table, sin_table], axis=1),
        groups,
    )
    grad_keys = lax.psum_scatter(grad_keys, "ctx", scatter_dimension=0, tiled=True)
    if lax.axis_size("tp") == 2:
        other = lax.ppermute(grad_keys, "tp", [(0, 1), (1, 0)])
        grad_keys = grad_keys.astype(jnp.float32) + other.astype(jnp.float32)
    else:
        grad_keys = lax.psum(grad_keys.astype(jnp.float32), "tp")
    grad_key_latent, grad_key_rope = grad_keys[:, :LAT], grad_keys[:, LAT:]
    part_grad_hidden, part_grad_next, coefficient = latent_backward(
        grad_key_latent,
        grad_key_rope,
        latent,
        inverse,
        inv_latent,
        gain_latent,
        positions,
        part_hidden,
        part_next,
    )
    grad_hidden = (
        gain_hidden
        * jnp.einsum("rc,dc->rd", part_grad_hidden, proj_hidden, preferred_element_type=jnp.float32)
        - coefficient[:, 0:1] * hidden_wide
    ).astype(jnp.bfloat16)
    grad_next = (
        gain_embed
        * jnp.einsum("rc,dc->rd", part_grad_next, proj_embed, preferred_element_type=jnp.float32)
        - coefficient[:, 1:2] * next_wide
    )
    grad_next_rounded = grad_next.astype(jnp.bfloat16)
    edge_grads = jnp.stack(
        [grad_next_rounded[tokens - 1], grad_next_rounded[half_rows - 1]], axis=0
    )
    returned = with_halo(edge_grads, (("ctx", 0),), 1)
    before_late = jnp.where(ctx_index == groups - 1, grad_next_rounded[half_rows - 1], returned[3])
    grad_embed = jnp.concatenate(
        [
            returned[0][None],
            grad_next_rounded[: half_rows - 1],
            before_late[None],
            grad_next_rounded[half_rows : tokens - 1],
        ],
        axis=0,
    )
    return (attended, grad_queries, grad_hidden, grad_embed)


def solution(mesh):
    placed = (
        P("ctx", "tp"),
        P("ctx", "tp"),
        P("tp"),
        P("tp"),
        P("tp", None),
        P("tp", None),
        P(),
        P(None, "tp"),
        P(None, "tp"),
        P("ctx", "tp"),
        P("ctx", "tp"),
    )
    return jax.shard_map(
        on_device,
        mesh=mesh,
        in_specs=placed,
        out_specs=(P("ctx", "tp"), P("ctx", "tp"), P("ctx", "tp"), P("ctx", "tp")),
        check_vma=False,
    )
```

time: 617 us -> 262 us (0.42)
  matrix products: 221 us -> 12.8 us
  local copies, waits for them, and re-layouts: 128 us -> 1.17 us
  Pallas kernels: 0 us -> 90.2 us
  other arithmetic: 84.5 us -> 5.76 us
  blocking collectives: 37.4 us -> 0 us
  waiting for transfers between devices: 114 us -> 122 us
    dot_general x69 -> x0, matrix products: 207 us -> none  [the longest x9 49.1 us: grad_step(): jnp.dot(grad_score, key_slab, preferred_element_type=jnp.float32)]
    pallas_call x0 -> x1, Pallas kernels: none -> 90.2 us  [attention(): pl.pallas_call(body, grid=(head_count // group,), in_specs=[whole(keys.sh...]
    slice x27 -> x0, local copies, waits for them, and re-layouts: 53.2 us -> none  [the longest x3 19.3 us: on_device(): query_full[rows_slice].reshape(half_rows * head_count, LAT + ROPE)]
    psum x2 -> x0, waiting for transfers between devices: 44.4 us -> none  [the longest x1 29.2 us: on_device(): lax.psum((part_hidden, part_next, squares), 'tp')]
    all_gather x1, waiting for transfers between devices: 0.01 us -> 44.2 us  [on_device(): lax.all_gather(jnp.concatenate([key_latent, key_rope], axis=1), 'ctx', ax...]
    another operation x10 -> x0, local copies, waits for them, and re-layouts: 29.3 us -> none
    reduce_sum x4 -> x0, other arithmetic: 27.7 us -> none  [the longest x2 16.1 us: attend_half(): jnp.sum(weights, axis=1, keepdims=True)]
    all_gather x1 -> x0, blocking collectives: 22.4 us -> none  [on_device(): lax.all_gather(key_rope, 'ctx', axis=0, tiled=True)]
  transfers between devices with their start and end apart: 9 -> 10, of which waited for: 6 -> 6; matrix products, arithmetic and copies ran while one was open for 18% -> 4% of each run, Pallas kernels for 0% -> 0%
where the time goes in v1:
time: 262 us
  waiting for transfers between devices  122 us (47%)
  Pallas kernels  90.2 us (34%)
  starting transfers between devices  15.5 us (6%)
  between operations  14.3 us (5%)
  matrix products  12.8 us (5%)
  other arithmetic  5.76 us (2%)
    pallas_call x1, Pallas kernels, attention(): pl.pallas_call(body, grid=(head_count // group,), in_specs=[whole(keys.sh...  90.2 us
    reduce_scatter x1, waiting for transfers between devices, on_device(): lax.psum_scatter(grad_keys, 'ctx', scatter_dimension=0, tiled=True)  63 us
    all_gather x1, waiting for transfers between devices, on_device(): lax.all_gather(jnp.concatenate([key_latent, key_rope], axis=1), 'ctx', ax...  44.2 us
    ppermute x3, waiting for transfers between devices, pair_sum(): return tuple((v + lax.ppermute(v, 'tp', [(0, 1), (1, 0)]) for v in values))  8.46 us
    ppermute x2, starting transfers between devices, with_halo(): before = lax.ppermute(last, axis, up)  6.04 us
  transfers between devices with their start and end apart: 10, of which 6 were waited for; matrix products, arithmetic and copies ran while one was open for 4% of the time, Pallas kernels for 0%

profile of v1, /device:TPU:0, one launch (start us, length us, event | category | flops | bytes accessed | tf_op | source)
XLA Modules:
  0.0 262.1 jit_solution(16111773016553994226)
XLA Ops:
  7.2 0.8 slice.67
  8.1 1.4 collective-permute-start
  9.5 4.0 %fusion.10 = f32[128,576]{1,0:T(8,128)S(1)} fusion(bf16[3584,576]{0,1:T(8,128)(2,1)} %param.15, bf16[128,3584]{1,0:T(8,128)(2,1)} %param.11, f32[3584]{0:T(1024)} %param.13), kind=kOutput, calls=%fused_computation.17 | convolution fusion | flops 529858560 | bytes 5355520 | tf_op jit(solution)/shard_map/dot_general | solution.py:387
  13.5 3.1 %collective-permute-start.3 = (f32[128,576]{1,0:T(8,128)S(1)}, f32[128,576]{1,0:T(8,128)S(1)}, u32[]{:S(2)}, u32[]{:S(2)}) collective-permute-start(f32[128,576]{1,0:T(8,128)S(1)} %fusion.10), channel_id=1, source_target_pairs={{0,1},{1,0},{2,3},{3,2},{4,5},{5,4},{6,7},{7,6},{8,9},{9,8},{10,11... | collective-permute-start | bytes 884744 | tf_op jit(solution)/shard_map/ppermute | solution.py:354
  17.1 2.7 %collective-permute-start.1 = (bf16[1,3584]{1,0:T(2,128)(2,1)S(1)}, bf16[1,3584]{1,0:T(2,128)(2,1)S(1)}, u32[]{:S(2)}, u32[]{:S(2)}) collective-permute-start(bf16[1,3584]{1,0:T(2,128)(2,1)S(1)} %get-tuple-element.22), channel_id=1, source_target_pairs={{0,2},{2,4},{4,6},{6,8},{8,10},{10,12},{12,14},{14,16},{16,18},{18... | collective-permute-start | bytes 21512 | tf_op jit(solution)/shard_map/ppermute | solution.py:28
  19.9 0.8 collective-permute-done.1
  21.0 0.4 collective-permute-start.2
  21.4 3.7 %fusion.8 = f32[128,576]{1,0:T(8,128)S(1)} fusion(bf16[3584,576]{0,1:T(8,128)(2,1)} %param.16, f32[3584]{0:T(1024)S(1)} %copy-done.5, bf16[1,3584]{1,0:T(2,128)(2,1)S(1)} %collective-permute-done.1, bf16[63,3584]{1,0:T(8,128)(2,1)S(1)} %get-tuple-element.20, bf16[1,3584]{1,0:T(2,128)(2,1)S(1)} %get-tuple-element.21, bf16[63,3584]{1,0:T(8,128)(2,1)S(1)} %get-tuple-element.19), kind=kOutput, calls=%fused_computation.16 | convolution fusion | flops 533069824 | bytes 5355520 | tf_op jit(solution)/shard_map/dot_general | solution.py:388
  25.1 1.8 collective-permute-start.4
  27.0 8.5 %collective-permute-done.4 = f32[128,576]{1,0:T(8,128)S(1)} collective-permute-done((f32[128,576]{1,0:T(8,128)S(1)}, f32[128,576]{1,0:T(8,128)S(1)}, u32[]{:S(2)}, u32[]{:S(2)}) %collective-permute-start.4) | collective-permute-done | bytes 294944 | tf_op jit(solution)/shard_map/ppermute | solution.py:354
  36.1 0.8 pad_maximum_fusion.3
  36.9 0.8 pad_maximum_fusion.4
  37.7 44.2 %all-gather.2.cloned.1.call-done.keys_ref = bf16[2048,576]{1,0:T(8,128)(2,1)} async-done(((bf16[128,576]{1,0:T(8,128)(2,1)}), bf16[2048,576]{1,0:T(8,128)(2,1)}) %all-gather.2.cloned.1.call-update) | async-done | bytes 2359312 | tf_op jit(solution)/shard_map/all_gather | solution.py:394
  81.9 90.2 %attention.1 = (bf16[128,4096]{1,0:T(8,128)(2,1)}, bf16[128,6144]{1,0:T(8,128)(2,1)}, bf16[2048,576]{1,0:T(8,128)(2,1)}) custom-call(bf16[2048,576]{1,0:T(8,128)(2,1)} %all-gather.2.cloned.1.call-done.keys_ref, bf16[128,6144]{1,0:T(8,128)(2,1)} %queries_ref.1, bf16[128,4096]{1,0:T(8,128)(2,1)} %grad_out_ref.1, bf16[512,4096]{1,0:T(8,128)(2,1)} %key_up_ref.1, ...), custom_call_target="tpu_custom_call" | custom-call | tf_op jit(solution)/shard_map/attention/pallas_call | solution.py:311
  172.2 63.0 %reduce-scatter.2.cloned.1.call-done = bf16[128,576]{1,0:T(8,128)(2,1)} async-done(((bf16[2048,576]{1,0:T(8,128)(2,1)}), bf16[128,576]{1,0:T(8,128)(2,1)}) %reduce-scatter.2.cloned.1.call-update) | async-done | bytes 147472 | tf_op jit(solution)/shard_map/reduce_scatter | solution.py:408
  235.1 1.5 collective-permute-start.5
  236.6 4.0 %collective-permute-done.5 = bf16[128,576]{1,0:T(8,128)(2,1)S(1)} collective-permute-done((bf16[128,576]{1,0:T(8,128)(2,1)}, bf16[128,576]{1,0:T(8,128)(2,1)S(1)}, u32[]{:S(2)}, u32[]{:S(2)}) %collective-permute-start.5) | collective-permute-done | bytes 147488 | tf_op jit(solution)/shard_map/ppermute | solution.py:410
  240.7 1.0 convert_add_fusion
  242.5 3.3 %fusion.7 = bf16[128,3584]{1,0:T(8,128)(2,1)S(1)} fusion(f32[128]{0:T(128)S(1)} %get-tuple-element.27, bf16[3584,576]{0,1:T(8,128)(2,1)} %param.16, f32[3584]{0:T(1024)S(1)} %copy-done.5, f32[128]{0:T(128)S(1)} %get-tuple-element.32, f32[128,32]{1,0:T(8,128)S(1)} %get-tuple-element.24, f32[128,32]{1,0:T(8,128)S(1)} %get-tuple-element.23, ...), kind=kOutput, calls=%fused_computation.15 | convolution fusion | flops 534282240 | bytes 6274048 | tf_op jit(solution)/shard_map/rc,dc->rd/dot_general | solution.py:433
  245.8 1.3 collective-permute-start.7
  247.1 1.7 collective-permute-done.7
  248.9 3.3 %collective-permute-start.6 = (bf16[1,3584]{1,0:T(2,128)(2,1)S(1)}, bf16[1,3584]{1,0:T(2,128)(2,1)S(1)}, u32[]{:S(2)}, u32[]{:S(2)}) collective-permute-start(bf16[1,3584]{1,0:T(2,128)(2,1)S(1)} %get-tuple-element.15), channel_id=1, source_target_pairs={{0,2},{2,4},{4,6},{6,8},{8,10},{10,12},{12,14},{14,16},{16,18},{18... | collective-permute-start | bytes 21512 | tf_op jit(solution)/shard_map/ppermute | solution.py:28
  252.2 1.9 fusion.1
  254.1 1.2 pad_maximum_fusion.1
  (43 shorter events, 2.6 us)
Async XLA Ops:
  7.2 74.8 %all-gather.2.cloned.1.call-start = ((), (), s32[]{:S(2)}) async-start(), calls=%async_computation.1 | async-start | bytes 2785280 | tf_op jit(solution)/shard_map/all_gather | solution.py:394
  8.0 8.5 %copy-start.1 = (bf16[128,3584]{1,0:T(8,128)(2,1)S(1)}, bf16[128,3584]{1,0:T(8,128)(2,1)}, u32[]{:S(2)}) copy-start(bf16[128,3584]{1,0:T(8,128)(2,1)} %param.11) | copy-start | bytes 2752516
  8.1 8.8 %copy-start.2 = (bf16[128,3584]{1,0:T(8,128)(2,1)S(1)}, bf16[128,3584]{1,0:T(8,128)(2,1)}, u32[]{:S(2)}) copy-start(bf16[128,3584]{1,0:T(8,128)(2,1)} %param.12) | copy-start | bytes 2752516
  8.1 9.0 %collective-permute-start = (bf16[1,3584]{1,0:T(2,128)(2,1)S(1)}, bf16[1,3584]{1,0:T(2,128)(2,1)S(1)}, u32[]{:S(2)}, u32[]{:S(2)}) collective-permute-start(bf16[1,3584]{1,0:T(2,128)(2,1)S(1)} %slice.67), channel_id=1, source_target_pairs={{2,0},{4,2},{6,4},{8,6},{10,8},{12,10},{14,12},{16,14},{18,16},{20... | collective-permute-start | bytes 21512 | tf_op jit(solution)/shard_map/ppermute | solution.py:29
  13.5 7.9 %copy-start.5 = (f32[3584]{0:T(1024)S(1)}, f32[3584]{0:T(1024)}, u32[]{:S(2)}) copy-start(f32[3584]{0:T(1024)} %param.14) | copy-start | bytes 43012
  13.5 13.4 %collective-permute-start.3 = (f32[128,576]{1,0:T(8,128)S(1)}, f32[128,576]{1,0:T(8,128)S(1)}, u32[]{:S(2)}, u32[]{:S(2)}) collective-permute-start(f32[128,576]{1,0:T(8,128)S(1)} %fusion.10), channel_id=1, source_target_pairs={{0,1},{1,0},{2,3},{3,2},{4,5},{5,4},{6,7},{7,6},{8,9},{9,8},{10,11... | collective-permute-start | bytes 884744 | tf_op jit(solution)/shard_map/ppermute | solution.py:354
  17.1 3.6 %collective-permute-start.1 = (bf16[1,3584]{1,0:T(2,128)(2,1)S(1)}, bf16[1,3584]{1,0:T(2,128)(2,1)S(1)}, u32[]{:S(2)}, u32[]{:S(2)}) collective-permute-start(bf16[1,3584]{1,0:T(2,128)(2,1)S(1)} %get-tuple-element.22), channel_id=1, source_target_pairs={{0,2},{2,4},{4,6},{6,8},{8,10},{10,12},{12,14},{14,16},{16,18},{18... | collective-permute-start | bytes 21512 | tf_op jit(solution)/shard_map/ppermute | solution.py:28
  21.0 5.9 %collective-permute-start.2 = (f32[128,2]{0,1:T(2,128)S(1)}, f32[128,2]{0,1:T(2,128)S(1)}, u32[]{:S(2)}, u32[]{:S(2)}) collective-permute-start(f32[128,2]{0,1:T(2,128)S(1)} %pad_maximum_fusion.6), channel_id=1, source_target_pairs={{0,1},{1,0},{2,3},{3,2},{4,5},{5,4},{6,7},{7,6},{8,9},{9,8},{10,11... | collective-permute-start | bytes 3080 | tf_op jit(solution)/shard_map/ppermute | solution.py:354
  25.1 10.6 %copy-start.4 = (f32[512]{0:T(512)S(1)}, f32[512]{0:T(512)}, u32[]{:S(2)}) copy-start(f32[512]{0:T(512)} %param.17) | copy-start | bytes 6148
  25.1 10.3 %collective-permute-start.4 = (f32[128,576]{1,0:T(8,128)S(1)}, f32[128,576]{1,0:T(8,128)S(1)}, u32[]{:S(2)}, u32[]{:S(2)}) collective-permute-start(f32[128,576]{1,0:T(8,128)S(1)} %fusion.8), channel_id=1, source_target_pairs={{0,1},{1,0},{2,3},{3,2},{4,5},{5,4},{6,7},{7,6},{8,9},{9,8},{10,11... | collective-permute-start | bytes 884744 | tf_op jit(solution)/shard_map/ppermute | solution.py:354
  36.9 198.3 %reduce-scatter.2.cloned.1.call-start = ((), (), s32[]{:S(2)}) async-start(), calls=%async_computation.2 | async-start | bytes 2785280 | tf_op jit(solution)/shard_map/reduce_scatter | solution.py:408
  235.1 5.5 %collective-permute-start.5 = (bf16[128,576]{1,0:T(8,128)(2,1)}, bf16[128,576]{1,0:T(8,128)(2,1)S(1)}, u32[]{:S(2)}, u32[]{:S(2)}) collective-permute-start(bf16[128,576]{1,0:T(8,128)(2,1)} %reduce-scatter.2.cloned.1.call-done), channel_id=1, source_target_pairs={{0,1},{1,0},{2,3},{3,2},{4,5},{5,4},{6,7},{7,6},{8,9},{9,8},{10,11... | collective-permute-start | bytes 442376 | tf_op jit(solution)/shard_map/ppermute | solution.py:410
  242.4 9.7 %copy-start = (bf16[3584,576]{0,1:T(8,128)(2,1)S(1)}, bf16[3584,576]{0,1:T(8,128)(2,1)}, u32[]{:S(2)}) copy-start(bf16[3584,576]{0,1:T(8,128)(2,1)} %param.15) | copy-start | bytes 12386308
  245.7 6.5 %copy-start.3 = (f32[3584]{0:T(1024)S(1)}, f32[3584]{0:T(1024)}, u32[]{:S(2)}) copy-start(f32[3584]{0:T(1024)} %param.13) | copy-start | bytes 43012
  245.8 3.1 %collective-permute-start.7 = (bf16[1,3584]{1,0:T(2,128)(2,1)S(1)}, bf16[1,3584]{1,0:T(2,128)(2,1)S(1)}, u32[]{:S(2)}, u32[]{:S(2)}) collective-permute-start(bf16[1,3584]{1,0:T(2,128)(2,1)S(1)} %slice.91), channel_id=1, source_target_pairs={{2,0},{4,2},{6,4},{8,6},{10,8},{12,10},{14,12},{16,14},{18,16},{20... | collective-permute-start | bytes 21512 | tf_op jit(solution)/shard_map/ppermute | solution.py:29
  248.9 5.2 %collective-permute-start.6 = (bf16[1,3584]{1,0:T(2,128)(2,1)S(1)}, bf16[1,3584]{1,0:T(2,128)(2,1)S(1)}, u32[]{:S(2)}, u32[]{:S(2)}) collective-permute-start(bf16[1,3584]{1,0:T(2,128)(2,1)S(1)} %get-tuple-element.15), channel_id=1, source_target_pairs={{0,2},{2,4},{4,6},{6,8},{8,10},{10,12},{12,14},{14,16},{16,18},{18... | collective-permute-start | bytes 21512 | tf_op jit(solution)/shard_map/ppermute | solution.py:28
Sparse Core Ops, SparseCore 0:
  37.0 44.8 all-gather.1
  172.3 62.8 reduce-scatter.1

commit v2 on v1

--- a/solution.py
+++ b/solution.py
@@ -152,23 +152,28 @@
     tokens = queries_ref.shape[0]
     half_rows = tokens // 2
     rows = group * half_rows
-    key_total = keys_ref.shape[0]
+    key_total = table.shape[0]
     width = LAT + ROPE
     padded = table.shape[1]
     blocks = key_total // key_block
-    chunk_rows = [
-        (2 * c if c < groups else 2 * (2 * groups - 1 - c) + 1) * half_rows
+    quarter = half_rows // 2
+    pieces_of = [
+        (2 * c + part, (part, d % 2, y, (d // 2) % 2, d // 4))
         for c in range(2 * groups)
+        for y, d in [(0, c) if c < groups else (1, 2 * groups - 1 - c)]
+        for part in range(2)
     ]
 
     @pl.when(step == 0)
     def _():
         dkey_acc[...] = jnp.zeros_like(dkey_acc)
         query_rows[...] = jnp.zeros_like(query_rows)
-        for c, row in enumerate(chunk_rows):
-            chunk = keys_ref[row : row + half_rows, :]
-            pad = jnp.zeros((half_rows, padded - width), chunk.dtype)
-            table[c * half_rows : (c + 1) * half_rows, :] = jnp.concatenate([chunk, pad], axis=1)
+        for piece, slot in pieces_of:
+            chunk = keys_ref[slot]
+            pad = jnp.zeros((quarter, padded - width), chunk.dtype)
+            table[piece * quarter : (piece + 1) * quarter, :] = jnp.concatenate(
+                [chunk, pad], axis=1
+            )
 
         @pl.loop(0, blocks)
         def _(j):
@@ -287,9 +292,9 @@
 
     @pl.when(step == pl.num_programs(0) - 1)
     def _():
-        for c, row in enumerate(chunk_rows):
-            grad_keys_ref[row : row + half_rows, :] = dkey_acc[
-                c * half_rows : (c + 1) * half_rows, :width
+        for piece, slot in pieces_of:
+            grad_keys_ref[slot] = dkey_acc[
+                piece * quarter : (piece + 1) * quarter, :width
             ].astype(grad_keys_ref.dtype)
 
 
@@ -298,7 +303,7 @@
     half_rows = tokens // 2
     head_count = key_up.shape[1] // NOPE
     group = group_size(head_count)
-    key_total = keys.shape[0]
+    key_total = tokens * groups
     key_block = 256
     blocks = key_total // key_block
     padded = LAT + 2 * ROPE
@@ -306,7 +311,7 @@
     body = functools.partial(
         attention_kernel, groups, group, key_block, (NOPE + ROPE) ** (-0.5)
     )
-    whole = lambda shape: pl.BlockSpec(shape, lambda i: (0, 0), pipeline_mode=pl.Buffered(1))
+    whole = lambda shape: pl.BlockSpec(shape, lambda i: (0,) * len(shape), pipeline_mode=pl.Buffered(1))
     column = lambda height, width: pl.BlockSpec((height, group * width), lambda i: (0, i))
     return pl.pallas_call(
         body,
@@ -348,10 +353,195 @@
     )(keys, queries, grad_out, key_up, value_up, cos2, sin2)
 
 
-def pair_sum(values):
-    if lax.axis_size("tp") != 2:
-        return lax.psum(values, "tp")
-    return tuple(v + lax.ppermute(v, "tp", [(0, 1), (1, 0)]) for v in values)
+class Place:
+    def __init__(self):
+        index = lax.axis_index("ctx")
+        self.core = index % 2
+        self.x = (index // 2) % 2
+        self.z = index // 4
+        self.y = lax.axis_index("tp")
+        self.depth = lax.axis_size("ctx") // 4
+
+    def device(self, z=None, x=None, core=None, y=None):
+        z = self.z if z is None else z
+        x = self.x if x is None else x
+        core = self.core if core is None else core
+        y = self.y if y is None else y
+        return ((z * 2 + x) * 2 + core, y)
+
+    def partners(self):
+        others = [
+            self.device(z=(self.z + k) % self.depth) for k in range(1, self.depth)
+        ]
+        sides = [
+            self.device(x=1 - self.x),
+            self.device(y=1 - self.y),
+            self.device(core=1 - self.core),
+        ]
+        return others, sides
+
+    def greet(self):
+        others, sides = self.partners()
+        barrier = pltpu.get_barrier_semaphore()
+        for device in others + sides:
+            pl.semaphore_signal(
+                barrier, inc=1, device_id=device, device_id_type=pl.DeviceIdType.MESH
+            )
+        pl.semaphore_wait(barrier, len(others + sides))
+
+
+def sender(send_sem, recv_sem):
+    def send(slot, source, target, device):
+        copy = pltpu.make_async_remote_copy(
+            src_ref=source,
+            dst_ref=target,
+            send_sem=send_sem.at[slot],
+            recv_sem=recv_sem.at[slot],
+            device_id=device,
+            device_id_type=pl.DeviceIdType.MESH,
+        )
+        copy.start()
+        return copy
+
+    return send
+
+
+def gather_kernel(own_ref, full_ref, send_sem, recv_sem):
+    me = Place()
+    c, x, y, z = me.core, me.x, me.y, me.z
+    others, (across_x, across_y, sibling) = me.partners()
+    me.greet()
+    send = sender(send_sem, recv_sem)
+    base = len(others)
+    along = [
+        send(k, own_ref, full_ref.at[:, c, y, x, z], device) for k, device in enumerate(others)
+    ]
+    full_ref[:, c, y, x, z] = own_ref[...]
+    for copy in along:
+        copy.wait_recv()
+    line = full_ref.at[:, c, y, x]
+    a2 = send(base, full_ref.at[0, c, y, x], full_ref.at[0, c, y, x], across_x)
+    b2 = send(base + 1, full_ref.at[1, c, y, x], full_ref.at[1, c, y, x], across_y)
+    c1 = send(base + 2, line, line, sibling)
+    a2.wait_recv()
+    a3 = send(base + 3, full_ref.at[0, c, y], full_ref.at[0, c, y], across_y)
+    got = full_ref.at[0, c, y, 1 - x]
+    c2 = send(base + 4, got, got, sibling)
+    b2.wait_recv()
+    b3 = send(base + 5, full_ref.at[1, c, :, x], full_ref.at[1, c, :, x], across_x)
+    got = full_ref.at[1, c, 1 - y, x]
+    c3 = send(base + 6, got, got, sibling)
+    a3.wait_recv()
+    got = full_ref.at[0, c, 1 - y]
+    c4 = send(base + 7, got, got, sibling)
+    b3.wait_recv()
+    got = full_ref.at[1, c, :, 1 - x]
+    c5 = send(base + 8, got, got, sibling)
+    for copy in (c1, c2, c3, c4, c5):
+        copy.wait_recv()
+    for copy in along + [a2, b2, c1, a3, c2, b3, c3, c4, c5]:
+        copy.wait_send()
+
+
+def scatter_kernel(
+    part_ref, out_ref, got1, sum1, got2, sum2, got3, sum3, got4, send_sem, recv_sem
+):
+    me = Place()
+    c, x, y, z = me.core, me.x, me.y, me.z
+    others, (across_x, across_y, sibling) = me.partners()
+    me.greet()
+    send = sender(send_sem, recv_sem)
+    wide = lambda value: value.astype(jnp.float32)
+    add = lambda a, b: (wide(a) + wide(b)).astype(jnp.bfloat16)
+    base = len(others)
+    s0 = send(base, part_ref.at[0, 1 - c, 1 - y], got1.at[0, 1 - y], sibling)
+    s1 = send(base + 1, part_ref.at[1, 1 - c, :, 1 - x], got1.at[1, :, 1 - x], sibling)
+    s2 = send(base + 2, part_ref.at[0, 1 - c, y], got1.at[0, y], sibling)
+    s3 = send(base + 3, part_ref.at[1, 1 - c, :, x], got1.at[1, :, x], sibling)
+    s0.wait_recv()
+    sum1[0, 1 - y] = add(part_ref[0, c, 1 - y], got1[0, 1 - y])
+    a2 = send(base + 4, sum1.at[0, 1 - y], got2.at[0], across_y)
+    s1.wait_recv()
+    sum1[1, :, 1 - x] = add(part_ref[1, c, :, 1 - x], got1[1, :, 1 - x])
+    b2 = send(base + 5, sum1.at[1, :, 1 - x], got2.at[1], across_x)
+    s2.wait_recv()
+    sum1[0, y] = add(part_ref[0, c, y], got1[0, y])
+    s3.wait_recv()
+    sum1[1, :, x] = add(part_ref[1, c, :, x], got1[1, :, x])
+    a2.wait_recv()
+    sum2[0, 1 - x] = add(sum1[0, y, 1 - x], got2[0, 1 - x])
+    a3 = send(base + 6, sum2.at[0, 1 - x], got3.at[0], across_x)
+    b2.wait_recv()
+    sum2[1, 1 - y] = add(sum1[1, 1 - y, x], got2[1, 1 - y])
+    b3 = send(base + 7, sum2.at[1, 1 - y], got3.at[1], across_y)
+    sum2[0, x] = add(sum1[0, y, x], got2[0, x])
+    sum2[1, y] = add(sum1[1, y, x], got2[1, y])
+    a3.wait_recv()
+    sum3[0] = add(sum2[0, x], got3[0])
+    b3.wait_recv()
+    sum3[1] = add(sum2[1, y], got3[1])
+    along = [
+        send(k, sum3.at[:, (z + k + 1) % me.depth], got4.at[k], device)
+        for k, device in enumerate(others)
+    ]
+    total = wide(sum3[:, z])
+    for k, copy in enumerate(along):
+        copy.wait_recv()
+        total = total + wide(got4[k])
+    out_ref[...] = total
+    for copy in along + [s0, s1, s2, s3, a2, b2, a3, b3]:
+        copy.wait_send()
+
+
+def vmem_call(body, out_shape, scratch, identity, name):
+    return pl.pallas_call(
+        body,
+        out_shape=out_shape,
+        in_specs=[pl.BlockSpec(memory_space=pltpu.VMEM)],
+        out_specs=pl.BlockSpec(memory_space=pltpu.VMEM),
+        scratch_shapes=scratch,
+        compiler_params=pltpu.CompilerParams(
+            collective_id=identity, has_side_effects=True, vmem_limit_bytes=40 * 1024 * 1024
+        ),
+        name=name,
+    )
+
+
+def gather_keys(own):
+    depth = lax.axis_size("ctx") // 4
+    shape = (2, 2, 2, 2, depth) + own.shape[1:]
+    sems = pltpu.SemaphoreType.DMA((depth + 8,))
+    return vmem_call(
+        gather_kernel, jax.ShapeDtypeStruct(shape, own.dtype), [sems, sems], 0, "gather_keys"
+    )(own)
+
+
+def scatter_keys(parts):
+    depth = parts.shape[4]
+    block = parts.shape[5:]
+    sems = pltpu.SemaphoreType.DMA((depth + 7,))
+    buffer = lambda *lead: pltpu.VMEM(lead + block, parts.dtype)
+    scratch = [
+        buffer(2, 2, 2, depth),
+        buffer(2, 2, 2, depth),
+        buffer(2, 2, depth),
+        buffer(2, 2, depth),
+        buffer(2, depth),
+        buffer(2, depth),
+        buffer(depth - 1, 2),
+        sems,
+        sems,
+    ]
+    return vmem_call(
+        scatter_kernel,
+        jax.ShapeDtypeStruct((2,) + block, jnp.float32),
+        scratch,
+        1,
+        "scatter_keys",
+    )(parts)
+
+
+SWAP = [(0, 1), (1, 0)]
 
 
 def on_device(
@@ -387,14 +577,30 @@
     part_hidden = jnp.dot(scaled_hidden, proj_hidden, preferred_element_type=jnp.float32)
     part_next = jnp.dot(scaled_next, proj_embed, preferred_element_type=jnp.float32)
     positions = local_positions(tokens, ctx_index, groups)
-    part_hidden, part_next, squares = pair_sum((part_hidden, part_next, squares))
+    cos_table, sin_table = rotation(positions)
+    paired = lax.axis_size("tp") == 2
+    depth = groups // 4
+    quarter = half_rows // 2
+    if paired:
+        tp_index = lax.axis_index("tp")
+        half_of = lambda value, k: lax.dynamic_slice_in_dim(value, k * half_rows, half_rows, 0)
+        part_hidden, part_next, squares = (
+            half_of(v, tp_index) + lax.ppermute(half_of(v, 1 - tp_index), "tp", SWAP)
+            for v in (part_hidden, part_next, squares)
+        )
+        positions = half_of(positions, tp_index)
+    else:
+        part_hidden, part_next, squares = lax.psum((part_hidden, part_next, squares), "tp")
     key_latent, key_rope, latent, inverse, inv_latent = finish_latent(
         part_hidden, part_next, squares, gain_latent, positions
     )
-    keys = lax.all_gather(
-        jnp.concatenate([key_latent, key_rope], axis=1), "ctx", axis=0, tiled=True
-    )
-    cos_table, sin_table = rotation(positions)
+    keys = jnp.concatenate([key_latent, key_rope], axis=1)
+    if paired:
+        keys = gather_keys(keys.reshape(2, quarter, LAT + ROPE))
+    else:
+        keys = lax.all_gather(keys, "ctx", axis=0, tiled=True)
+        keys = keys.reshape(depth, 2, 2, 2, 2, quarter, LAT + ROPE)
+        keys = keys.transpose(4, 2, 3, 1, 0, 5, 6)
     attended, grad_queries, grad_keys = attention(
         keys,
         queries,
@@ -405,11 +611,11 @@
         jnp.concatenate([sin_table, sin_table], axis=1),
         groups,
     )
-    grad_keys = lax.psum_scatter(grad_keys, "ctx", scatter_dimension=0, tiled=True)
-    if lax.axis_size("tp") == 2:
-        other = lax.ppermute(grad_keys, "tp", [(0, 1), (1, 0)])
-        grad_keys = grad_keys.astype(jnp.float32) + other.astype(jnp.float32)
+    if paired:
+        grad_keys = scatter_keys(grad_keys).reshape(half_rows, LAT + ROPE)
     else:
+        grad_keys = grad_keys.transpose(4, 3, 1, 2, 0, 5, 6).reshape(-1, LAT + ROPE)
+        grad_keys = lax.psum_scatter(grad_keys, "ctx", scatter_dimension=0, tiled=True)
         grad_keys = lax.psum(grad_keys.astype(jnp.float32), "tp")
     grad_key_latent, grad_key_rope = grad_keys[:, :LAT], grad_keys[:, LAT:]
     part_grad_hidden, part_grad_next, coefficient = latent_backward(
@@ -423,6 +629,17 @@
         part_hidden,
         part_next,
     )
+    if paired:
+
+        def both_halves(value):
+            other = lax.ppermute(value, "tp", SWAP)
+            early = jnp.where(tp_index == 0, value, other)
+            late = jnp.where(tp_index == 0, other, value)
+            return jnp.concatenate([early, late], axis=0)
+
+        part_grad_hidden = both_halves(part_grad_hidden)
+        part_grad_next = both_halves(part_grad_next)
+        coefficient = both_halves(coefficient)
     grad_hidden = (
         gain_hidden
         * jnp.einsum("rc,dc->rd", part_grad_hidden, proj_hidden, preferred_element_type=jnp.float32)

time: 262 us -> 198 us (0.76)
  waiting for transfers between devices: 122 us -> 13.4 us
  Pallas kernels: 90.2 us -> 142 us
  between operations: 14.3 us -> 0.96 us
  local copies, waits for them, and re-layouts: 1.17 us -> 6.04 us
    reduce_scatter x1 -> x0, waiting for transfers between devices: 63 us -> none  [on_device(): lax.psum_scatter(grad_keys, 'ctx', scatter_dimension=0, tiled=True)]
    pallas_call x0 -> x2, Pallas kernels: none -> 53.2 us  [the longest x1 27.1 us: gather_keys(): vmem_call(gather_kernel, jax.ShapeDtypeStruct(shape, own.dtype), [sems, s...]
    all_gather x1 -> x0, waiting for transfers between devices: 44.2 us -> none  [on_device(): lax.all_gather(jnp.concatenate([key_latent, key_rope], axis=1), 'ctx', ax...]
    unnamed x12 -> x21, local copies, waits for them, and re-layouts: 0.04 us -> 3.6 us
    ppermute x4 -> x6, waiting for transfers between devices: 12.5 us -> 11 us  [the longest x3 7.9 us: on_device(): lax.ppermute(half_of(v, 1 - tp_index), 'tp', SWAP)]
    ppermute x4 -> x6, starting transfers between devices: 6.71 us -> 7.39 us  [the longest x3 5.09 us: on_device(): lax.ppermute(half_of(v, 1 - tp_index), 'tp', SWAP)]
  transfers between devices with their start and end apart: 10 -> 10, of which waited for: 6 -> 5; matrix products, arithmetic and copies ran while one was open for 4% -> 8% of each run, Pallas kernels for 0% -> 0%
where the time goes in v2:
time: 198 us; the launch traced here: 197 us
  Pallas kernels  142 us (72%)
  starting transfers between devices  17.2 us (9%)
  waiting for transfers between devices  13.4 us (7%)
  matrix products  12.4 us (6%)
  local copies, waits for them, and re-layouts  6.04 us (3%)
  other arithmetic  5.51 us (3%)
    pallas_call x1, Pallas kernels, attention(): pl.pallas_call(body, grid=(head_count // group,), in_specs=[whole(keys.sh...  88.4 us
    pallas_call x1, Pallas kernels, gather_keys(): vmem_call(gather_kernel, jax.ShapeDtypeStruct(shape, own.dtype), [sems, s...  27.1 us
    pallas_call x1, Pallas kernels, scatter_keys(): vmem_call(scatter_kernel, jax.ShapeDtypeStruct((2,) + block, jnp.float32)...  26.1 us
    ppermute x3, waiting for transfers between devices, on_device(): lax.ppermute(half_of(v, 1 - tp_index), 'tp', SWAP)  7.9 us
    ppermute x2, starting transfers between devices, with_halo(): before = lax.ppermute(last, axis, up)  7.21 us
    ppermute x3, starting transfers between devices, on_device(): lax.ppermute(half_of(v, 1 - tp_index), 'tp', SWAP)  5.09 us
  transfers between devices with their start and end apart: 10, of which 5 were waited for; matrix products, arithmetic and copies ran while one was open for 8% of the time, Pallas kernels for 0%

profile of v2, /device:TPU:0, one launch (start us, length us, event | category | flops | bytes accessed | tf_op | source)
XLA Modules:
  0.0 197.1 jit_solution(11211481204780278259)
XLA Ops:
  0.6 0.8 slice.67
  1.5 1.3 collective-permute-start
  2.8 3.8 %fusion.10 = f32[128,576]{0,1:T(8,128)S(1)} fusion(bf16[3584,576]{0,1:T(8,128)(2,1)} %param.15, bf16[128,3584]{1,0:T(8,128)(2,1)} %param.11, f32[3584]{0:T(1024)} %param.13), kind=kOutput, calls=%fused_computation.17 | convolution fusion | flops 529858560 | bytes 5355520 | tf_op jit(solution)/shard_map/dot_general | solution.py:577
  6.6 0.9 constant_dynamic-slice_fusion.1
  7.4 3.0 %collective-permute-start.3 = (f32[64,576]{0,1:T(8,128)}, f32[64,576]{0,1:T(8,128)S(1)}, u32[]{:S(2)}, u32[]{:S(2)}) collective-permute-start(f32[64,576]{0,1:T(8,128)} %constant_dynamic-slice_fusion.1), channel_id=1, source_target_pairs={{0,1},{1,0},{2,3},{3,2},{4,5},{5,4},{6,7},{7,6},{8,9},{9,8},{10,11... | collective-permute-start | bytes 442376 | tf_op jit(solution)/shard_map/ppermute | solution.py:588
  12.1 2.8 %collective-permute-start.1 = (bf16[1,3584]{1,0:T(2,128)(2,1)S(1)}, bf16[1,3584]{1,0:T(2,128)(2,1)S(1)}, u32[]{:S(2)}, u32[]{:S(2)}) collective-permute-start(bf16[1,3584]{1,0:T(2,128)(2,1)S(1)} %get-tuple-element.21), channel_id=1, source_target_pairs={{0,2},{2,4},{4,6},{6,8},{8,10},{10,12},{12,14},{14,16},{16,18},{18... | collective-permute-start | bytes 21512 | tf_op jit(solution)/shard_map/ppermute | solution.py:28
  16.4 3.4 %fusion.8 = f32[128,576]{0,1:T(8,128)S(1)} fusion(bf16[3584,576]{0,1:T(8,128)(2,1)} %param.16, f32[3584]{0:T(1024)S(1)} %copy-done.8, bf16[1,3584]{1,0:T(2,128)(2,1)S(1)} %collective-permute-done.1, bf16[63,3584]{1,0:T(8,128)(2,1)S(1)} %get-tuple-element.19, bf16[1,3584]{1,0:T(2,128)(2,1)S(1)} %get-tuple-element.20, bf16[63,3584]{1,0:T(8,128)(2,1)S(1)} %get-tuple-element.18), kind=kOutput, calls=%fused_computation.16 | convolution fusion | flops 533069824 | bytes 5355520 | tf_op jit(solution)/shard_map/dot_general | solution.py:578
  20.0 1.7 collective-permute-start.4
  21.8 7.9 %collective-permute-done.4 = f32[64,576]{0,1:T(8,128)S(1)} collective-permute-done((f32[64,576]{0,1:T(8,128)S(1)}, f32[64,576]{0,1:T(8,128)S(1)}, u32[]{:S(2)}, u32[]{:S(2)}) %collective-permute-start.4) | collective-permute-done | bytes 147488 | tf_op jit(solution)/shard_map/ppermute | solution.py:588
  30.6 27.1 %gather_keys.1.keys_ref = bf16[2,2,2,2,4,32,576]{6,5,4,3,2,1,0:T(8,128)(2,1)S(1)} custom-call(bf16[2,32,576]{2,1,0:T(8,128)(2,1)S(1)} %bitcast.20), custom_call_target="tpu_custom_call" | custom-call | tf_op jit(solution)/shard_map/gather_keys/pallas_call | solution.py:514
  57.7 1.5 copy-done
  59.2 88.4 %attention.1 = (bf16[128,4096]{1,0:T(8,128)(2,1)}, bf16[128,6144]{1,0:T(8,128)(2,1)}, bf16[2,2,2,2,4,32,576]{6,5,4,3,2,1,0:T(8,128)(2,1)}) custom-call(bf16[2,2,2,2,4,32,576]{6,5,4,3,2,1,0:T(8,128)(2,1)} %copy-done, bf16[128,6144]{1,0:T(8,128)(2,1)} %queries_ref.1, bf16[128,4096]{1,0:T(8,128)(2,1)} %grad_out_ref.1, bf16[512,4096]{1,0:T(8,128)(2,1)} %key_up_ref.1, ...), custom_call_target="tpu_custom_call" | custom-call | tf_op jit(solution)/shard_map/attention/pallas_call | solution.py:316
  147.6 1.7 copy-done.1
  149.3 26.1 %scatter_keys.1 = f32[2,32,576]{2,1,0:T(8,128)S(1)} custom-call(bf16[2,2,2,2,4,32,576]{6,5,4,3,2,1,0:T(8,128)(2,1)S(1)} %copy-done.1), custom_call_target="tpu_custom_call" | custom-call | tf_op jit(solution)/shard_map/scatter_keys/pallas_call | solution.py:535
  176.3 1.2 multiply_reduce_fusion.1
  177.8 1.8 collective-permute-start.7
  179.8 1.3 collective-permute-done.6
  181.2 1.7 collective-permute-done.7
  183.0 3.3 %fusion.3 = bf16[128,3584]{1,0:T(8,128)(2,1)S(1)} fusion(bf16[3584,576]{0,1:T(8,128)(2,1)} %param.16, f32[128]{0:T(128)S(1)} %get-tuple-element.36, f32[3584]{0:T(1024)S(1)} %copy-done.8, bf16[64,576]{0,1:T(8,128)(2,1)S(1)} %get-tuple-element.25, bf16[64,576]{0,1:T(8,128)(2,1)S(1)} %get-tuple-element.24, bf16[1,3584]{1,0:T(2,128)(2,1)S(1)} %collective-permute-done.1, ...), kind=kOutput, calls=%fused_computation.5 | convolution fusion | flops 534282240 | bytes 6126080 | tf_op jit(solution)/shard_map/rc,dc->rd/dot_general | solution.py:650
  186.4 1.3 collective-permute-start.9
  187.8 1.7 collective-permute-done.9
  189.6 4.5 %collective-permute-start.8 = (bf16[1,3584]{1,0:T(2,128)(2,1)S(1)}, bf16[1,3584]{1,0:T(2,128)(2,1)S(1)}, u32[]{:S(2)}, u32[]{:S(2)}) collective-permute-start(bf16[1,3584]{1,0:T(2,128)(2,1)S(1)} %get-tuple-element.14), channel_id=1, source_target_pairs={{0,2},{2,4},{4,6},{6,8},{8,10},{10,12},{12,14},{14,16},{16,18},{18... | collective-permute-start | bytes 21512 | tf_op jit(solution)/shard_map/ppermute | solution.py:28
  194.0 1.9 fusion.2
  196.0 1.2 pad_maximum_fusion.1
  (63 shorter events, 5.9 us)
Async XLA Ops:
  1.5 10.6 %collective-permute-start = (bf16[1,3584]{1,0:T(2,128)(2,1)S(1)}, bf16[1,3584]{1,0:T(2,128)(2,1)S(1)}, u32[]{:S(2)}, u32[]{:S(2)}) collective-permute-start(bf16[1,3584]{1,0:T(2,128)(2,1)S(1)} %slice.67), channel_id=1, source_target_pairs={{2,0},{4,2},{6,4},{8,6},{10,8},{12,10},{14,12},{16,14},{18,16},{20... | collective-permute-start | bytes 21512 | tf_op jit(solution)/shard_map/ppermute | solution.py:29
  2.8 7.7 %copy-start.3 = (bf16[128,3584]{1,0:T(8,128)(2,1)S(1)}, bf16[128,3584]{1,0:T(8,128)(2,1)}, u32[]{:S(2)}) copy-start(bf16[128,3584]{1,0:T(8,128)(2,1)} %param.11) | copy-start | bytes 2752516
  6.6 4.2 %copy-start.5 = (bf16[128,3584]{1,0:T(8,128)(2,1)S(1)}, bf16[128,3584]{1,0:T(8,128)(2,1)}, u32[]{:S(2)}) copy-start(bf16[128,3584]{1,0:T(8,128)(2,1)} %param.12) | copy-start | bytes 2752516
  7.4 14.4 %collective-permute-start.3 = (f32[64,576]{0,1:T(8,128)}, f32[64,576]{0,1:T(8,128)S(1)}, u32[]{:S(2)}, u32[]{:S(2)}) collective-permute-start(f32[64,576]{0,1:T(8,128)} %constant_dynamic-slice_fusion.1), channel_id=1, source_target_pairs={{0,1},{1,0},{2,3},{3,2},{4,5},{5,4},{6,7},{7,6},{8,9},{9,8},{10,11... | collective-permute-start | bytes 442376 | tf_op jit(solution)/shard_map/ppermute | solution.py:588
  10.7 5.7 %copy-start.8 = (f32[3584]{0:T(1024)S(1)}, f32[3584]{0:T(1024)}, u32[]{:S(2)}) copy-start(f32[3584]{0:T(1024)} %param.14) | copy-start | bytes 43012
  12.1 3.6 %collective-permute-start.1 = (bf16[1,3584]{1,0:T(2,128)(2,1)S(1)}, bf16[1,3584]{1,0:T(2,128)(2,1)S(1)}, u32[]{:S(2)}, u32[]{:S(2)}) collective-permute-start(bf16[1,3584]{1,0:T(2,128)(2,1)S(1)} %get-tuple-element.21), channel_id=1, source_target_pairs={{0,2},{2,4},{4,6},{6,8},{8,10},{10,12},{12,14},{14,16},{16,18},{18... | collective-permute-start | bytes 21512 | tf_op jit(solution)/shard_map/ppermute | solution.py:28
  16.1 5.7 %collective-permute-start.2 = (f32[64,2]{0,1:T(2,128)S(1)}, f32[64,2]{0,1:T(2,128)S(1)}, u32[]{:S(2)}, u32[]{:S(2)}) collective-permute-start(f32[64,2]{0,1:T(2,128)S(1)} %constant_dynamic-slice_fusion.2), channel_id=1, source_target_pairs={{0,1},{1,0},{2,3},{3,2},{4,5},{5,4},{6,7},{7,6},{8,9},{9,8},{10,11... | collective-permute-start | bytes 1544 | tf_op jit(solution)/shard_map/ppermute | solution.py:588
  19.9 10.3 %copy-start.7 = (f32[512]{0:T(512)S(1)}, f32[512]{0:T(512)}, u32[]{:S(2)}) copy-start(f32[512]{0:T(512)} %param.17) | copy-start | bytes 6148
  20.0 9.7 %collective-permute-start.4 = (f32[64,576]{0,1:T(8,128)S(1)}, f32[64,576]{0,1:T(8,128)S(1)}, u32[]{:S(2)}, u32[]{:S(2)}) collective-permute-start(f32[64,576]{0,1:T(8,128)S(1)} %constant_dynamic-slice_fusion), channel_id=1, source_target_pairs={{0,1},{1,0},{2,3},{3,2},{4,5},{5,4},{6,7},{7,6},{8,9},{9,8},{10,11... | collective-permute-start | bytes 442376 | tf_op jit(solution)/shard_map/ppermute | solution.py:588
  29.7 0.7 copy-start.4
  57.7 1.5 copy-start
  147.6 1.7 copy-start.1
  177.5 3.6 %collective-permute-start.6 = (f32[64,2]{0,1:T(2,128)S(1)}, f32[64,2]{0,1:T(2,128)S(1)}, u32[]{:S(2)}, u32[]{:S(2)}) collective-permute-start(f32[64,2]{0,1:T(2,128)S(1)} %fusion.39), channel_id=1, source_target_pairs={{0,1},{1,0},{2,3},{3,2},{4,5},{5,4},{6,7},{7,6},{8,9},{9,8},{10,11... | collective-permute-start | bytes 1544 | tf_op jit(solution)/shard_map/ppermute | solution.py:635
  177.8 5.2 %collective-permute-start.7 = (bf16[64,576]{0,1:T(8,128)(2,1)S(1)}, bf16[64,576]{0,1:T(8,128)(2,1)S(1)}, u32[]{:S(2)}, u32[]{:S(2)}) collective-permute-start(bf16[64,576]{0,1:T(8,128)(2,1)S(1)} %get-tuple-element.26), channel_id=1, source_target_pairs={{0,1},{1,0},{2,3},{3,2},{4,5},{5,4},{6,7},{7,6},{8,9},{9,8},{10,11... | collective-permute-start | bytes 221192 | tf_op jit(solution)/shard_map/ppermute | solution.py:635
  179.6 8.2 %collective-permute-start.5 = (bf16[64,576]{0,1:T(8,128)(2,1)S(1)}, bf16[64,576]{0,1:T(8,128)(2,1)S(1)}, u32[]{:S(2)}, u32[]{:S(2)}) collective-permute-start(bf16[64,576]{0,1:T(8,128)(2,1)S(1)} %get-tuple-element.29), channel_id=1, source_target_pairs={{0,1},{1,0},{2,3},{3,2},{4,5},{5,4},{6,7},{7,6},{8,9},{9,8},{10,11... | collective-permute-start | bytes 221192 | tf_op jit(solution)/shard_map/ppermute | solution.py:635
  183.0 11.1 %copy-start.2 = (bf16[3584,576]{0,1:T(8,128)(2,1)S(1)}, bf16[3584,576]{0,1:T(8,128)(2,1)}, u32[]{:S(2)}) copy-start(bf16[3584,576]{0,1:T(8,128)(2,1)} %param.15) | copy-start | bytes 12386308
  186.3 7.7 %copy-start.6 = (f32[3584]{0:T(1024)S(1)}, f32[3584]{0:T(1024)}, u32[]{:S(2)}) copy-start(f32[3584]{0:T(1024)} %param.13) | copy-start | bytes 43012
  186.4 3.1 %collective-permute-start.9 = (bf16[1,3584]{1,0:T(2,128)(2,1)S(1)}, bf16[1,3584]{1,0:T(2,128)(2,1)S(1)}, u32[]{:S(2)}, u32[]{:S(2)}) collective-permute-start(bf16[1,3584]{1,0:T(2,128)(2,1)S(1)} %slice.91), channel_id=1, source_target_pairs={{2,0},{4,2},{6,4},{8,6},{10,8},{12,10},{14,12},{16,14},{18,16},{20... | collective-permute-start | bytes 21512 | tf_op jit(solution)/shard_map/ppermute | solution.py:29
  189.6 6.4 %collective-permute-start.8 = (bf16[1,3584]{1,0:T(2,128)(2,1)S(1)}, bf16[1,3584]{1,0:T(2,128)(2,1)S(1)}, u32[]{:S(2)}, u32[]{:S(2)}) collective-permute-start(bf16[1,3584]{1,0:T(2,128)(2,1)S(1)} %get-tuple-element.14), channel_id=1, source_target_pairs={{0,2},{2,4},{4,6},{6,8},{8,10},{10,12},{12,14},{14,16},{16,18},{18... | collective-permute-start | bytes 21512 | tf_op jit(solution)/shard_map/ppermute | solution.py:28

commit v3 on v2

--- a/solution.py
+++ b/solution.py
@@ -116,8 +116,11 @@
     return (part_grad_hidden, part_grad_next, coefficient)
 
 
+UNROLL = 3
+
+
 def group_size(head_count):
-    for size in (4, 2, 1):
+    for size in (8, 4, 2, 1):
         if head_count % size == 0:
             return size
 
@@ -146,6 +149,7 @@
     out_acc,
     dquery_acc,
     dkey_acc,
+    row_stat,
 ):
     step = pl.program_id(0)
     ctx_index = lax.axis_index("ctx")
@@ -208,87 +212,124 @@
             query_rows[h, target, LAT : LAT + ROPE] = rotated[source]
             grad_rows[h, target, :] = grads[source]
 
+    lanes = 128
+    spans = key_block // lanes
+    early_pos = ctx_index * half_rows
+    late_pos = (2 * groups - 1 - ctx_index) * half_rows
+    early_count = (early_pos + half_rows + key_block - 1) // key_block
+    tiles = blocks + 1
+    unroll = UNROLL if tiles % UNROLL == 0 else 1
+    row_off = lax.broadcasted_iota(jnp.int32, (rows, lanes), 0) % half_rows
+    gap = row_off - lax.broadcasted_iota(jnp.int32, (rows, lanes), 1)
+
+    def locate(tile):
+        late = (tile >= early_count).astype(jnp.int32)
+        block = tile - late * early_count
+        return late, block, pl.multiple_of(block * key_block, key_block)
+
+    def over_tiles(body):
+        @pl.loop(0, tiles // unroll)
+        def _(trip):
+            for k in range(unroll):
+                body(trip * unroll + k)
+
+    row_stat[0] = jnp.full(row_stat.shape[1:], -1e30, jnp.float32)
+    row_stat[1] = jnp.zeros(row_stat.shape[1:], jnp.float32)
+    row_stat[2] = jnp.zeros(row_stat.shape[1:], jnp.float32)
+    out_acc[...] = jnp.zeros_like(out_acc)
+    dquery_acc[...] = jnp.zeros_like(dquery_acc)
+
+    def score_tile(tile):
+        late, block, first = locate(tile)
+        shift = first - jnp.where(late == 1, late_pos, early_pos)
+        scores = jnp.dot(query_rows[late], table_t[block], preferred_element_type=jnp.float32)
+        running = row_stat[0, late]
+        for k in range(spans):
+            part = scores[:, k * lanes : (k + 1) * lanes]
+            part = jnp.where(gap >= shift + k * lanes, part, -1e30)
+            score_buf[tile, :, k * lanes : (k + 1) * lanes] = part
+            running = jnp.maximum(running, part)
+        row_stat[0, late] = running
+        dprob_buf[tile] = jnp.dot(
+            grad_rows[late], table_t[block, :LAT, :], preferred_element_type=jnp.float32
+        )
+
+    over_tiles(score_tile)
     for h in range(2):
-        first_pos = (ctx_index if h == 0 else 2 * groups - 1 - ctx_index) * half_rows
-        block_count = (first_pos + half_rows + key_block - 1) // key_block
-        row_pos = first_pos + lax.broadcasted_iota(jnp.int32, (rows, key_block), 0) % half_rows
-        key_off = lax.broadcasted_iota(jnp.int32, (rows, key_block), 1)
-        gap = row_pos - key_off
-        lanes = 128
-
-        def fold(values, op):
-            total = values[:, :lanes]
-            for k in range(1, key_block // lanes):
-                total = op(total, values[:, k * lanes : (k + 1) * lanes])
-            return total
-
-        def score_step(j, running):
-            scores = jnp.dot(query_rows[h], table_t[j], preferred_element_type=jnp.float32)
-            scores = jnp.where(gap >= j * key_block, scores, -1e30)
-            score_buf[j] = scores
-            dprob_buf[j] = jnp.dot(
-                grad_rows[h], table_t[j, :LAT, :], preferred_element_type=jnp.float32
+        row_stat[0, h] = jnp.broadcast_to(
+            jnp.max(row_stat[0, h], axis=1, keepdims=True), (rows, lanes)
+        )
+
+    def weight_tile(tile):
+        late, block, first = locate(tile)
+        row_max = row_stat[0, late]
+        weight_sum = row_stat[1, late]
+        delta_sum = row_stat[2, late]
+        for k in range(spans):
+            span = slice(k * lanes, (k + 1) * lanes)
+            weights = jnp.exp((score_buf[tile, :, span] - row_max) * score_scale)
+            score_buf[tile, :, span] = weights
+            weight_sum = weight_sum + weights
+            delta_sum = delta_sum + weights * dprob_buf[tile, :, span]
+        row_stat[1, late] = weight_sum
+        row_stat[2, late] = delta_sum
+
+    over_tiles(weight_tile)
+    for h in range(2):
+        inv_sum = 1.0 / jnp.sum(row_stat[1, h], axis=1, keepdims=True)
+        delta = jnp.sum(row_stat[2, h], axis=1, keepdims=True) * inv_sum
+        row_stat[1, h] = jnp.broadcast_to(inv_sum, (rows, lanes))
+        row_stat[2, h] = jnp.broadcast_to(delta, (rows, lanes))
+
+    def grad_tile(tile):
+        late, block, first = locate(tile)
+        inv_sum = row_stat[1, late]
+        delta = row_stat[2, late]
+        probs = []
+        dscores = []
+        for k in range(spans):
+            span = slice(k * lanes, (k + 1) * lanes)
+            prob = (score_buf[tile, :, span] * inv_sum).astype(jnp.bfloat16)
+            probs.append(prob)
+            dscores.append(
+                (
+                    prob.astype(jnp.float32) * (dprob_buf[tile, :, span] - delta) * score_scale
+                ).astype(jnp.bfloat16)
             )
-            return jnp.maximum(running, fold(scores, jnp.maximum))
-
-        running = lax.fori_loop(
-            0, block_count, score_step, jnp.full((rows, lanes), -1e30, jnp.float32)
+        prob = jnp.concatenate(probs, axis=1)
+        dscore = jnp.concatenate(dscores, axis=1)
+        keys = table[pl.ds(first, key_block), :]
+        out_acc[late] += jnp.dot(prob, keys[:, :LAT], preferred_element_type=jnp.float32)
+        dquery_acc[late] += jnp.dot(dscore, keys, preferred_element_type=jnp.float32)
+        dkey_lead = lax.dot_general(
+            dscore, query_rows[late, :, :LAT], tn, preferred_element_type=jnp.float32
+        ) + lax.dot_general(prob, grad_rows[late], tn, preferred_element_type=jnp.float32)
+        dkey_acc[pl.ds(first, key_block), :LAT] += dkey_lead
+        dkey_acc[pl.ds(first, key_block), LAT:] += lax.dot_general(
+            dscore, query_rows[late, :, LAT:], tn, preferred_element_type=jnp.float32
         )
-        row_max = jnp.max(running, axis=1, keepdims=True)
-
-        def weight_step(j, sums):
-            weights = jnp.exp((score_buf[j] - row_max) * score_scale)
-            score_buf[j] = weights
-            return (
-                sums[0] + fold(weights, jnp.add),
-                sums[1] + fold(weights * dprob_buf[j], jnp.add),
+
+    over_tiles(grad_tile)
+    pieces = []
+    for g in range(group):
+        part = slice(g * half_rows, (g + 1) * half_rows)
+        both = lambda ref, span: jnp.concatenate([ref[0, part, span], ref[1, part, span]], axis=0)
+        attended_ref[:, g * VDIM : (g + 1) * VDIM] = jnp.dot(
+            both(out_acc, slice(0, LAT)).astype(jnp.bfloat16),
+            value_up_ref[:, g * VDIM : (g + 1) * VDIM],
+            preferred_element_type=jnp.float32,
+        ).astype(jnp.bfloat16)
+        pieces.append(
+            jnp.dot(
+                both(dquery_acc, slice(0, LAT)).astype(jnp.bfloat16),
+                key_up_ref[:, g * NOPE : (g + 1) * NOPE],
+                preferred_element_type=jnp.float32,
             )
-
-        zeros = jnp.zeros((rows, lanes), jnp.float32)
-        weight_sum, delta_sum = lax.fori_loop(0, block_count, weight_step, (zeros, zeros))
-        inv_sum = 1.0 / jnp.sum(weight_sum, axis=1, keepdims=True)
-        delta = jnp.sum(delta_sum, axis=1, keepdims=True) * inv_sum
-        out_acc[...] = jnp.zeros_like(out_acc)
-        dquery_acc[...] = jnp.zeros_like(dquery_acc)
-
-        def grad_step(j, carry):
-            first = pl.multiple_of(j * key_block, key_block)
-            prob = (score_buf[j] * inv_sum).astype(jnp.bfloat16)
-            dscore = (
-                prob.astype(jnp.float32) * (dprob_buf[j] - delta) * score_scale
-            ).astype(jnp.bfloat16)
-            keys = table[pl.ds(first, key_block), :]
-            out_acc[...] += jnp.dot(prob, keys[:, :LAT], preferred_element_type=jnp.float32)
-            dquery_acc[...] += jnp.dot(dscore, keys, preferred_element_type=jnp.float32)
-            dkey_acc[pl.ds(first, key_block), :] += lax.dot_general(
-                dscore, query_rows[h], tn, preferred_element_type=jnp.float32
-            )
-            dkey_acc[pl.ds(first, key_block), :LAT] += lax.dot_general(
-                prob, grad_rows[h], tn, preferred_element_type=jnp.float32
-            )
-            return carry
-
-        lax.fori_loop(0, block_count, grad_step, 0)
-        token = slice(h * half_rows, (h + 1) * half_rows)
-        pieces = []
-        for g in range(group):
-            part = slice(g * half_rows, (g + 1) * half_rows)
-            attended_ref[token, g * VDIM : (g + 1) * VDIM] = jnp.dot(
-                out_acc[part, :].astype(jnp.bfloat16),
-                value_up_ref[:, g * VDIM : (g + 1) * VDIM],
-                preferred_element_type=jnp.float32,
-            ).astype(jnp.bfloat16)
-            pieces.append(
-                jnp.dot(
-                    dquery_acc[part, :LAT].astype(jnp.bfloat16),
-                    key_up_ref[:, g * NOPE : (g + 1) * NOPE],
-                    preferred_element_type=jnp.float32,
-                )
-            )
-            tail = dquery_acc[part, LAT : LAT + ROPE]
-            swapped = jnp.concatenate([tail[:, half:], -tail[:, :half]], axis=1)
-            pieces.append(tail * cos2[token] + swapped * sin2[token])
-        grad_queries_ref[token, :] = jnp.concatenate(pieces, axis=1).astype(jnp.bfloat16)
+        )
+        tail = both(dquery_acc, slice(LAT, LAT + ROPE))
+        swapped = jnp.concatenate([tail[:, half:], -tail[:, :half]], axis=1)
+        pieces.append(tail * cos2 + swapped * sin2)
+    grad_queries_ref[...] = jnp.concatenate(pieces, axis=1).astype(jnp.bfloat16)
 
     @pl.when(step == pl.num_programs(0) - 1)
     def _():
@@ -340,11 +381,12 @@
             pltpu.VMEM((blocks, padded, key_block), jnp.bfloat16),
             pltpu.VMEM((2, rows, padded), jnp.bfloat16),
             pltpu.VMEM((2, rows, LAT), jnp.bfloat16),
-            pltpu.VMEM((blocks, rows, key_block), jnp.float32),
-            pltpu.VMEM((blocks, rows, key_block), jnp.float32),
-            pltpu.VMEM((rows, LAT), jnp.float32),
-            pltpu.VMEM((rows, padded), jnp.float32),
+            pltpu.VMEM((blocks + 1, rows, key_block), jnp.float32),
+            pltpu.VMEM((blocks + 1, rows, key_block), jnp.float32),
+            pltpu.VMEM((2, rows, LAT), jnp.float32),
+            pltpu.VMEM((2, rows, padded), jnp.float32),
             pltpu.VMEM((key_total, padded), jnp.float32),
+            pltpu.VMEM((3, 2, rows, 128), jnp.float32),
         ],
         compiler_params=pltpu.CompilerParams(
             dimension_semantics=("arbitrary",), vmem_limit_bytes=60 * 1024 * 1024

time: 198 us -> 176 us (0.89)
  Pallas kernels: 142 us -> 120 us
    pallas_call x1, Pallas kernels: 88.4 us -> 66.5 us  [attention(): pl.pallas_call(body, grid=(head_count // group,), in_specs=[whole(keys.sh...]
  transfers between devices with their start and end apart: 10 -> 10, of which waited for: 5 -> 5; matrix products, arithmetic and copies ran while one was open for 8% -> 9% of each run, Pallas kernels for 0% -> 0%
where the time goes in v3:
time: 176 us; the launch traced here: 175 us
  Pallas kernels  120 us (68%)
  starting transfers between devices  17.2 us (10%)
  waiting for transfers between devices  13.4 us (8%)
  matrix products  12.4 us (7%)
  local copies, waits for them, and re-layouts  6.04 us (3%)
  other arithmetic  5.51 us (3%)
    pallas_call x1, Pallas kernels, attention(): pl.pallas_call(body, grid=(head_count // group,), in_specs=[whole(keys.sh...  66.5 us
    pallas_call x1, Pallas kernels, gather_keys(): vmem_call(gather_kernel, jax.ShapeDtypeStruct(shape, own.dtype), [sems, s...  27.1 us
    pallas_call x1, Pallas kernels, scatter_keys(): vmem_call(scatter_kernel, jax.ShapeDtypeStruct((2,) + block, jnp.float32)...  26.2 us
    ppermute x3, waiting for transfers between devices, on_device(): lax.ppermute(half_of(v, 1 - tp_index), 'tp', SWAP)  7.88 us
    ppermute x2, starting transfers between devices, with_halo(): before = lax.ppermute(last, axis, up)  7.15 us
    ppermute x3, starting transfers between devices, on_device(): lax.ppermute(half_of(v, 1 - tp_index), 'tp', SWAP)  5.1 us
    dot_general x1, matrix products, on_device(): jnp.dot(scaled_hidden, proj_hidden, preferred_element_type=jnp.float32)  3.77 us
    unnamed x21, local copies, waits for them, and re-layouts  3.6 us
  transfers between devices with their start and end apart: 10, of which 5 were waited for; matrix products, arithmetic and copies ran while one was open for 9% of the time, Pallas kernels for 0%

profile of v3, /device:TPU:0, one launch (start us, length us, event | category | flops | bytes accessed | tf_op | source)
XLA Modules:
  0.0 175.3 jit_solution(7067053471154783965)
XLA Ops:
  0.6 0.8 slice.67
  1.5 1.3 collective-permute-start
  2.8 3.8 %fusion.10 = f32[128,576]{0,1:T(8,128)S(1)} fusion(bf16[3584,576]{0,1:T(8,128)(2,1)} %param.15, bf16[128,3584]{1,0:T(8,128)(2,1)} %param.11, f32[3584]{0:T(1024)} %param.13), kind=kOutput, calls=%fused_computation.17 | convolution fusion | flops 529858560 | bytes 5355520 | tf_op jit(solution)/shard_map/dot_general | solution.py:619
  6.6 0.9 constant_dynamic-slice_fusion.1
  7.4 3.0 %collective-permute-start.3 = (f32[64,576]{0,1:T(8,128)}, f32[64,576]{0,1:T(8,128)S(1)}, u32[]{:S(2)}, u32[]{:S(2)}) collective-permute-start(f32[64,576]{0,1:T(8,128)} %constant_dynamic-slice_fusion.1), channel_id=1, source_target_pairs={{0,1},{1,0},{2,3},{3,2},{4,5},{5,4},{6,7},{7,6},{8,9},{9,8},{10,11... | collective-permute-start | bytes 442376 | tf_op jit(solution)/shard_map/ppermute | solution.py:630
  12.1 2.8 %collective-permute-start.1 = (bf16[1,3584]{1,0:T(2,128)(2,1)S(1)}, bf16[1,3584]{1,0:T(2,128)(2,1)S(1)}, u32[]{:S(2)}, u32[]{:S(2)}) collective-permute-start(bf16[1,3584]{1,0:T(2,128)(2,1)S(1)} %get-tuple-element.21), channel_id=1, source_target_pairs={{0,2},{2,4},{4,6},{6,8},{8,10},{10,12},{12,14},{14,16},{16,18},{18... | collective-permute-start | bytes 21512 | tf_op jit(solution)/shard_map/ppermute | solution.py:28
  16.4 3.4 %fusion.8 = f32[128,576]{0,1:T(8,128)S(1)} fusion(bf16[3584,576]{0,1:T(8,128)(2,1)} %param.16, f32[3584]{0:T(1024)S(1)} %copy-done.8, bf16[1,3584]{1,0:T(2,128)(2,1)S(1)} %collective-permute-done.1, bf16[63,3584]{1,0:T(8,128)(2,1)S(1)} %get-tuple-element.19, bf16[1,3584]{1,0:T(2,128)(2,1)S(1)} %get-tuple-element.20, bf16[63,3584]{1,0:T(8,128)(2,1)S(1)} %get-tuple-element.18), kind=kOutput, calls=%fused_computation.16 | convolution fusion | flops 533069824 | bytes 5355520 | tf_op jit(solution)/shard_map/dot_general | solution.py:620
  20.0 1.7 collective-permute-start.4
  21.8 7.9 %collective-permute-done.4 = f32[64,576]{0,1:T(8,128)S(1)} collective-permute-done((f32[64,576]{0,1:T(8,128)S(1)}, f32[64,576]{0,1:T(8,128)S(1)}, u32[]{:S(2)}, u32[]{:S(2)}) %collective-permute-start.4) | collective-permute-done | bytes 147488 | tf_op jit(solution)/shard_map/ppermute | solution.py:630
  30.6 27.1 %gather_keys.1.keys_ref = bf16[2,2,2,2,4,32,576]{6,5,4,3,2,1,0:T(8,128)(2,1)S(1)} custom-call(bf16[2,32,576]{2,1,0:T(8,128)(2,1)S(1)} %bitcast.20), custom_call_target="tpu_custom_call" | custom-call | tf_op jit(solution)/shard_map/gather_keys/pallas_call | solution.py:556
  57.7 1.5 copy-done
  59.1 66.5 %attention.1 = (bf16[128,4096]{1,0:T(8,128)(2,1)}, bf16[128,6144]{1,0:T(8,128)(2,1)}, bf16[2,2,2,2,4,32,576]{6,5,4,3,2,1,0:T(8,128)(2,1)}) custom-call(bf16[2,2,2,2,4,32,576]{6,5,4,3,2,1,0:T(8,128)(2,1)} %copy-done, bf16[128,6144]{1,0:T(8,128)(2,1)} %queries_ref.1, bf16[128,4096]{1,0:T(8,128)(2,1)} %grad_out_ref.1, bf16[512,4096]{1,0:T(8,128)(2,1)} %key_up_ref.1, ...), custom_call_target="tpu_custom_call" | custom-call | tf_op jit(solution)/shard_map/attention/pallas_call | solution.py:357
  125.7 1.7 copy-done.1
  127.4 26.2 %scatter_keys.1 = f32[2,32,576]{2,1,0:T(8,128)S(1)} custom-call(bf16[2,2,2,2,4,32,576]{6,5,4,3,2,1,0:T(8,128)(2,1)S(1)} %copy-done.1), custom_call_target="tpu_custom_call" | custom-call | tf_op jit(solution)/shard_map/scatter_keys/pallas_call | solution.py:577
  154.5 1.2 multiply_reduce_fusion.1
  156.0 1.8 %collective-permute-start.7 = (bf16[64,576]{0,1:T(8,128)(2,1)S(1)}, bf16[64,576]{0,1:T(8,128)(2,1)S(1)}, u32[]{:S(2)}, u32[]{:S(2)}) collective-permute-start(bf16[64,576]{0,1:T(8,128)(2,1)S(1)} %get-tuple-element.26), channel_id=1, source_target_pairs={{0,1},{1,0},{2,3},{3,2},{4,5},{5,4},{6,7},{7,6},{8,9},{9,8},{10,11... | collective-permute-start | bytes 221192 | tf_op jit(solution)/shard_map/ppermute | solution.py:677
  158.0 1.3 collective-permute-done.6
  159.4 1.8 %collective-permute-done.7 = bf16[64,576]{0,1:T(8,128)(2,1)S(1)} collective-permute-done((bf16[64,576]{0,1:T(8,128)(2,1)S(1)}, bf16[64,576]{0,1:T(8,128)(2,1)S(1)}, u32[]{:S(2)}, u32[]{:S(2)}) %collective-permute-start.7) | collective-permute-done | bytes 73760 | tf_op jit(solution)/shard_map/ppermute | solution.py:677
  161.2 3.4 %fusion.3 = bf16[128,3584]{1,0:T(8,128)(2,1)S(1)} fusion(bf16[3584,576]{0,1:T(8,128)(2,1)} %param.16, f32[128]{0:T(128)S(1)} %get-tuple-element.36, f32[3584]{0:T(1024)S(1)} %copy-done.8, bf16[64,576]{0,1:T(8,128)(2,1)S(1)} %get-tuple-element.25, bf16[64,576]{0,1:T(8,128)(2,1)S(1)} %get-tuple-element.24, bf16[1,3584]{1,0:T(2,128)(2,1)S(1)} %collective-permute-done.1, ...), kind=kOutput, calls=%fused_computation.5 | convolution fusion | flops 534282240 | bytes 6126080 | tf_op jit(solution)/shard_map/rc,dc->rd/dot_general | solution.py:692
  164.7 1.3 collective-permute-start.9
  166.0 1.7 collective-permute-done.9
  167.8 4.4 %collective-permute-start.8 = (bf16[1,3584]{1,0:T(2,128)(2,1)S(1)}, bf16[1,3584]{1,0:T(2,128)(2,1)S(1)}, u32[]{:S(2)}, u32[]{:S(2)}) collective-permute-start(bf16[1,3584]{1,0:T(2,128)(2,1)S(1)} %get-tuple-element.14), channel_id=1, source_target_pairs={{0,2},{2,4},{4,6},{6,8},{8,10},{10,12},{12,14},{14,16},{16,18},{18... | collective-permute-start | bytes 21512 | tf_op jit(solution)/shard_map/ppermute | solution.py:28
  172.2 1.9 %fusion.2 = bf16[128,3584]{1,0:T(8,128)(2,1)} fusion(bf16[3584,576]{0,1:T(8,128)(2,1)S(1)} %copy-done.2, bf16[128,3584]{1,0:T(8,128)(2,1)S(1)} %copy-done.3, f32[128]{0:T(128)S(1)} %get-tuple-element.37, f32[3584]{0:T(1024)S(1)} %copy-done.6, bf16[64,576]{0,1:T(8,128)(2,1)S(1)} %get-tuple-element.28, bf16[64,576]{0,1:T(8,128)(2,1)S(1)} %get-tuple-element.27), kind=kOutput, calls=%fused_computation.4 | convolution fusion | flops 531070976 | bytes 6126080 | tf_op jit(solution)/shard_map/rc,dc->rd/dot_general | solution.py:687
  174.2 1.2 pad_maximum_fusion.1
  (63 shorter events, 5.9 us)
Async XLA Ops:
  1.5 10.6 %collective-permute-start = (bf16[1,3584]{1,0:T(2,128)(2,1)S(1)}, bf16[1,3584]{1,0:T(2,128)(2,1)S(1)}, u32[]{:S(2)}, u32[]{:S(2)}) collective-permute-start(bf16[1,3584]{1,0:T(2,128)(2,1)S(1)} %slice.67), channel_id=1, source_target_pairs={{2,0},{4,2},{6,4},{8,6},{10,8},{12,10},{14,12},{16,14},{18,16},{20... | collective-permute-start | bytes 21512 | tf_op jit(solution)/shard_map/ppermute | solution.py:29
  2.8 7.7 %copy-start.3 = (bf16[128,3584]{1,0:T(8,128)(2,1)S(1)}, bf16[128,3584]{1,0:T(8,128)(2,1)}, u32[]{:S(2)}) copy-start(bf16[128,3584]{1,0:T(8,128)(2,1)} %param.11) | copy-start | bytes 2752516
  6.6 4.2 %copy-start.5 = (bf16[128,3584]{1,0:T(8,128)(2,1)S(1)}, bf16[128,3584]{1,0:T(8,128)(2,1)}, u32[]{:S(2)}) copy-start(bf16[128,3584]{1,0:T(8,128)(2,1)} %param.12) | copy-start | bytes 2752516
  7.4 14.4 %collective-permute-start.3 = (f32[64,576]{0,1:T(8,128)}, f32[64,576]{0,1:T(8,128)S(1)}, u32[]{:S(2)}, u32[]{:S(2)}) collective-permute-start(f32[64,576]{0,1:T(8,128)} %constant_dynamic-slice_fusion.1), channel_id=1, source_target_pairs={{0,1},{1,0},{2,3},{3,2},{4,5},{5,4},{6,7},{7,6},{8,9},{9,8},{10,11... | collective-permute-start | bytes 442376 | tf_op jit(solution)/shard_map/ppermute | solution.py:630
  10.7 5.7 %copy-start.8 = (f32[3584]{0:T(1024)S(1)}, f32[3584]{0:T(1024)}, u32[]{:S(2)}) copy-start(f32[3584]{0:T(1024)} %param.14) | copy-start | bytes 43012
  12.1 3.6 %collective-permute-start.1 = (bf16[1,3584]{1,0:T(2,128)(2,1)S(1)}, bf16[1,3584]{1,0:T(2,128)(2,1)S(1)}, u32[]{:S(2)}, u32[]{:S(2)}) collective-permute-start(bf16[1,3584]{1,0:T(2,128)(2,1)S(1)} %get-tuple-element.21), channel_id=1, source_target_pairs={{0,2},{2,4},{4,6},{6,8},{8,10},{10,12},{12,14},{14,16},{16,18},{18... | collective-permute-start | bytes 21512 | tf_op jit(solution)/shard_map/ppermute | solution.py:28
  16.0 5.7 %collective-permute-start.2 = (f32[64,2]{0,1:T(2,128)S(1)}, f32[64,2]{0,1:T(2,128)S(1)}, u32[]{:S(2)}, u32[]{:S(2)}) collective-permute-start(f32[64,2]{0,1:T(2,128)S(1)} %constant_dynamic-slice_fusion.2), channel_id=1, source_target_pairs={{0,1},{1,0},{2,3},{3,2},{4,5},{5,4},{6,7},{7,6},{8,9},{9,8},{10,11... | collective-permute-start | bytes 1544 | tf_op jit(solution)/shard_map/ppermute | solution.py:630
  19.9 10.3 %copy-start.7 = (f32[512]{0:T(512)S(1)}, f32[512]{0:T(512)}, u32[]{:S(2)}) copy-start(f32[512]{0:T(512)} %param.17) | copy-start | bytes 6148
  20.0 9.7 %collective-permute-start.4 = (f32[64,576]{0,1:T(8,128)S(1)}, f32[64,576]{0,1:T(8,128)S(1)}, u32[]{:S(2)}, u32[]{:S(2)}) collective-permute-start(f32[64,576]{0,1:T(8,128)S(1)} %constant_dynamic-slice_fusion), channel_id=1, source_target_pairs={{0,1},{1,0},{2,3},{3,2},{4,5},{5,4},{6,7},{7,6},{8,9},{9,8},{10,11... | collective-permute-start | bytes 442376 | tf_op jit(solution)/shard_map/ppermute | solution.py:630
  29.7 0.7 copy-start.4
  57.6 1.5 copy-start
  125.7 1.7 copy-start.1
  155.7 3.6 %collective-permute-start.6 = (f32[64,2]{0,1:T(2,128)S(1)}, f32[64,2]{0,1:T(2,128)S(1)}, u32[]{:S(2)}, u32[]{:S(2)}) collective-permute-start(f32[64,2]{0,1:T(2,128)S(1)} %fusion.39), channel_id=1, source_target_pairs={{0,1},{1,0},{2,3},{3,2},{4,5},{5,4},{6,7},{7,6},{8,9},{9,8},{10,11... | collective-permute-start | bytes 1544 | tf_op jit(solution)/shard_map/ppermute | solution.py:677
  156.0 5.2 %collective-permute-start.7 = (bf16[64,576]{0,1:T(8,128)(2,1)S(1)}, bf16[64,576]{0,1:T(8,128)(2,1)S(1)}, u32[]{:S(2)}, u32[]{:S(2)}) collective-permute-start(bf16[64,576]{0,1:T(8,128)(2,1)S(1)} %get-tuple-element.26), channel_id=1, source_target_pairs={{0,1},{1,0},{2,3},{3,2},{4,5},{5,4},{6,7},{7,6},{8,9},{9,8},{10,11... | collective-permute-start | bytes 221192 | tf_op jit(solution)/shard_map/ppermute | solution.py:677
  157.8 8.2 %collective-permute-start.5 = (bf16[64,576]{0,1:T(8,128)(2,1)S(1)}, bf16[64,576]{0,1:T(8,128)(2,1)S(1)}, u32[]{:S(2)}, u32[]{:S(2)}) collective-permute-start(bf16[64,576]{0,1:T(8,128)(2,1)S(1)} %get-tuple-element.29), channel_id=1, source_target_pairs={{0,1},{1,0},{2,3},{3,2},{4,5},{5,4},{6,7},{7,6},{8,9},{9,8},{10,11... | collective-permute-start | bytes 221192 | tf_op jit(solution)/shard_map/ppermute | solution.py:677
  161.2 11.0 %copy-start.2 = (bf16[3584,576]{0,1:T(8,128)(2,1)S(1)}, bf16[3584,576]{0,1:T(8,128)(2,1)}, u32[]{:S(2)}) copy-start(bf16[3584,576]{0,1:T(8,128)(2,1)} %param.15) | copy-start | bytes 12386308
  164.6 7.6 %copy-start.6 = (f32[3584]{0:T(1024)S(1)}, f32[3584]{0:T(1024)}, u32[]{:S(2)}) copy-start(f32[3584]{0:T(1024)} %param.13) | copy-start | bytes 43012
  164.7 3.1 %collective-permute-start.9 = (bf16[1,3584]{1,0:T(2,128)(2,1)S(1)}, bf16[1,3584]{1,0:T(2,128)(2,1)S(1)}, u32[]{:S(2)}, u32[]{:S(2)}) collective-permute-start(bf16[1,3584]{1,0:T(2,128)(2,1)S(1)} %slice.91), channel_id=1, source_target_pairs={{2,0},{4,2},{6,4},{8,6},{10,8},{12,10},{14,12},{16,14},{18,16},{20... | collective-permute-start | bytes 21512 | tf_op jit(solution)/shard_map/ppermute | solution.py:29
  167.8 6.3 %collective-permute-start.8 = (bf16[1,3584]{1,0:T(2,128)(2,1)S(1)}, bf16[1,3584]{1,0:T(2,128)(2,1)S(1)}, u32[]{:S(2)}, u32[]{:S(2)}) collective-permute-start(bf16[1,3584]{1,0:T(2,128)(2,1)S(1)} %get-tuple-element.14), channel_id=1, source_target_pairs={{0,2},{2,4},{4,6},{6,8},{8,10},{10,12},{12,14},{14,16},{16,18},{18... | collective-permute-start | bytes 21512 | tf_op jit(solution)/shard_map/ppermute | solution.py:28
